TPU v7x, 128 devices: a whole 4x4x4 slice. The times are simulated.
128 devices in a mesh: row: 8 (over x, core), col: 16 (over y, z).
Axes of the slice: x: 4, y: 4, z: 4, core: 2. Of those that a mesh axis runs over, the one named last changes fastest.
Arguments:
- adjacency: bfloat16 [8192, 65536], P('row', 'col'), may hold values from -0.03125 to 0.03125
- tile_mask: int32 [32, 256], P('row', 'col'), may hold values from 0 to 1, as said below
- operand: bfloat16 [65536, 2048], P('col'), may hold values from -6 to 6
- current: bfloat16 [8192, 2048], P('row', 'col'), may hold values from 0 to 1
Outputs:
- reached: bfloat16 [8192, 2048], P('row', 'col')
- progress: float32 [32], P('row')
Inputs may be any that keep to these rules, and one draw needn't show every extreme that they name: Split tile_mask into blocks of 4 tile rows by 16 tile columns, aligned to multiples of these. Every block holds at least one nonzero tile, and a block together with the block in the same tile columns whose tile rows start 16 tile rows farther down (upper half of the slab paired with lower half, in order) holds exactly 64 nonzero tiles.
All inputs are finite; a program needn't handle non-finite values.
Results may differ from a plain program's by a relative error of at most 0.0045.
Values may be sent and summed in bfloat16 or wider, within the bound.
No kernel may reach another device: no remote copies, remote signals or barrier semaphores. Data moves between devices by JAX's collectives and lax.ppermute only.
A program may use at most 128 MiB of HBM per device.

v0:
```python
import jax
import jax.numpy as jnp
from jax import lax
from jax.sharding import Mesh
from jax.sharding import PartitionSpec as P

TILE = 256
COL = ("col_0", "col_1")


def summed_rows(shard, axes, dim):
    for axis in axes:
        shard = lax.psum_scatter(shard, axis, scatter_dimension=dim, tiled=True)
    return shard


def copy_for_each(shard, axis):
    size = lax.axis_size(axis)
    return lax.all_to_all(
        jnp.broadcast_to(shard[None], (size, *shard.shape)), axis, 0, 0, tiled=True
    )


def over_copies(shard, axis):
    everything = copy_for_each(shard, axis)
    return jnp.sum(everything, axis=0)


def combined_pairwise(pieces, combine):
    while len(jax.tree.leaves(pieces)[0]) > 1:
        pieces = jax.vmap(combine)(*(pieces[side::2] for side in (0, 1)))
    return pieces[0]


def entering(shard, axis, combine, identity):
    size, mine = (lax.axis_size(axis), lax.axis_index(axis))
    passed = jnp.arange(size) < mine

    def kept(part, zero, own):
        part = jnp.where(
            passed.reshape(-1, *(1 for _ in own.shape)), part, jnp.asarray(zero, own.dtype)
        )
        return part

    pieces = copy_for_each(shard, axis)
    return combined_pairwise(kept(pieces, identity, shard), combine)


def add_pair(earlier, later):
    return earlier + later


def local(adjacency, tile_mask, operand, current):
    row_count, col_count = adjacency.shape
    tiles_rows = row_count // TILE
    tiles_cols = col_count // TILE
    keep_tile = tile_mask.astype(jnp.bfloat16)[:, None, :, None]
    masked = (adjacency.reshape(tiles_rows, TILE, tiles_cols, TILE) * keep_tile).reshape(
        row_count, col_count
    )
    partial_value = jnp.dot(masked, operand, preferred_element_type=jnp.float32)
    own_width = current.shape[1]
    logits = summed_rows(partial_value.astype(jnp.bfloat16), COL, 1).astype(jnp.float32)
    prior_value = current.astype(jnp.float32)
    lifted = (1.0 - prior_value) * jax.nn.sigmoid(logits)
    reached = (prior_value + lifted).astype(jnp.bfloat16)
    window = own_width * lax.axis_size(COL)
    local_gain = jnp.sum(lifted.reshape(tiles_rows, TILE * own_width), axis=1) / (TILE * window)
    row_gains = over_copies(local_gain, COL)
    before = entering(jnp.sum(row_gains), "row", add_pair, jnp.float32(0.0))
    progress = before + jnp.cumsum(row_gains)
    return (reached, progress)


def solution(mesh):
    torus = Mesh(mesh.devices.reshape(mesh.shape["row"], 4, 4), ("row", "col_0", "col_1"))
    in_specs = (P("row", COL), P("row", COL), P(COL, None), P("row", COL))
    out_specs = (P("row", COL), P("row"))
    return jax.shard_map(local, mesh=torus, in_specs=in_specs, out_specs=out_specs, check_vma=False)
```

profile of v0, /device:TPU:1, one launch (start us, length us, event | category | flops | bytes accessed | tf_op | source)
XLA Modules:
  0.0 163.0 jit_solution(18415871693937537983)
XLA Ops:
  7.2 0.0 reduce-scatter.5.cloned.1.call-start
  7.2 0.7 convert_element_type.16
  7.9 3.8 %mul.14 = bf16[4,256,16,256]{3,2,1,0:T(8,128)(2,1)} broadcast(bf16[4,16]{1,0:T(4,128)(2,1)S(1)} %convert_element_type.16), dimensions={0,2} | broadcast | bytes 8388736 | tf_op jit(solution)/shard_map/mul | solution.py:58
  11.7 12.2 %copy.12 = bf16[128,8,16,256]{3,1,2,0:T(8,128)(2,1)} copy(bf16[128,8,16,256]{3,2,1,0:T(8,128)(2,1)} %bitcast.10) | data formatting | bytes 16777216
  24.0 0.0 copy-start
  24.0 26.1 %fusion.2 = bf16[1024,2048]{1,0:T(8,128)(2,1)} fusion(bf16[4096,2048]{1,0:T(8,128)(2,1)} %param.6, bf16[1024,4096]{1,0:T(8,128)(2,1)} %param.4, bf16[1024,4096]{1,0:T(8,128)(2,1)} %bitcast.11), kind=kOutput, calls=%fused_computation.2 | convolution fusion | flops 17186160640 | bytes 37748736 | tf_op jit(solution)/shard_map/dot_general | solution.py:61
  50.0 0.0 reduce-scatter.5.cloned.1.call-update
  50.0 0.0 reduce-scatter.7.cloned.1.call-start
  50.1 50.2 %reduce-scatter.5.cloned.1.call-done = bf16[1024,512]{1,0:T(8,128)(2,1)} async-done(((bf16[1024,2048]{1,0:T(8,128)(2,1)}), bf16[1024,512]{1,0:T(8,128)(2,1)}) %reduce-scatter.5.cloned.1.call-update) | async-done | bytes 1048592 | tf_op jit(solution)/shard_map/reduce_scatter | solution.py:13
  100.3 2.3 %copy.8 = bf16[1024,512]{0,1:T(8,128)(2,1)} copy(bf16[1024,512]{1,0:T(8,128)(2,1)} %reduce-scatter.5.cloned.1.call-done) | data formatting | bytes 2097152
  102.6 0.0 reduce-scatter.7.cloned.1.call-update
  102.6 22.3 %reduce-scatter.7.cloned.1.call-done = bf16[128,1024]{1,0:T(8,128)(2,1)} async-done(((bf16[512,1024]{1,0:T(8,128)(2,1)}), bf16[128,1024]{1,0:T(8,128)(2,1)}) %reduce-scatter.7.cloned.1.call-update) | async-done | bytes 262160
  124.9 1.1 copy.9
  126.0 0.0 copy-done
  126.0 0.9 fusion.7
  126.9 0.1 reduce_sum.36
  127.0 0.6 broadcast_in_dim.7
  127.7 4.7 %all-to-all-start = ((f32[16,1,4]{2,1,0:T(1,128)}), f32[16,1,4]{2,1,0:T(1,128)S(1)}, u32[]{:S(2)}, u32[]{:S(2)}) async-start(f32[16,1,4]{2,1,0:T(1,128)} %broadcast_in_dim.7), calls=%async_computation.1 | async-start | bytes 16384 | tf_op jit(solution)/shard_map/all_to_all | solution.py:19
  132.4 6.4 %all-to-all-done = f32[16,1,4]{2,1,0:T(1,128)S(1)} async-done(((f32[16,1,4]{2,1,0:T(1,128)}), f32[16,1,4]{2,1,0:T(1,128)S(1)}, u32[]{:S(2)}, u32[]{:S(2)}) %all-to-all-start) | async-done | bytes 288 | tf_op jit(solution)/shard_map/all_to_all | solution.py:19
  138.8 0.6 fusion.8
  139.4 1.2 broadcast_in_dim.8
  140.7 8.0 %all-to-all-start.1 = ((f32[8,1,1]{2,1,0:T(1,128)}), f32[8,1,1]{2,1,0:T(1,128)S(1)}, u32[]{:S(2)}, u32[]{:S(2)}) async-start(f32[8,1,1]{2,1,0:T(1,128)} %broadcast_in_dim.8), calls=%async_computation.2 | async-start | bytes 8192 | tf_op jit(solution)/shard_map/all_to_all | solution.py:19
  148.6 0.2 reduce-window.9
  148.8 4.4 %all-to-all-done.1 = f32[8,1,1]{2,1,0:T(1,128)S(1)} async-done(((f32[8,1,1]{2,1,0:T(1,128)}), f32[8,1,1]{2,1,0:T(1,128)S(1)}, u32[]{:S(2)}, u32[]{:S(2)}) %all-to-all-start.1) | async-done | bytes 64 | tf_op jit(solution)/shard_map/all_to_all | solution.py:19
  153.2 0.1 reduce.5
  153.3 0.1 slice.20
  153.4 0.1 slice.21
  153.5 0.1 slice.22
  153.6 0.1 slice.23
  153.7 0.6 fusion.9
  155.7 0.5 add_bitcast_fusion
  (5 shorter events, 0.0 us)
Async XLA Ops:
  7.2 93.1 %reduce-scatter.5.cloned.1.call-start = ((), (), s32[]{:S(2)}) async-start(), calls=%async_computation.4 | async-start | bytes 5242880 | tf_op jit(solution)/shard_map/reduce_scatter | solution.py:13
  24.0 102.1 %copy-start = (bf16[1024,128]{1,0:T(8,128)(2,1)S(1)}, bf16[1024,128]{1,0:T(8,128)(2,1)}, u32[]{:S(2)}) copy-start(bf16[1024,128]{1,0:T(8,128)(2,1)} %param.7) | copy-start | bytes 786436
  50.0 74.8 %reduce-scatter.7.cloned.1.call-start = ((), (), s32[]{:S(2)}) async-start(), calls=%async_computation.5 | async-start | bytes 1310720
  127.7 11.1 %all-to-all-start = ((f32[16,1,4]{2,1,0:T(1,128)}), f32[16,1,4]{2,1,0:T(1,128)S(1)}, u32[]{:S(2)}, u32[]{:S(2)}) async-start(f32[16,1,4]{2,1,0:T(1,128)} %broadcast_in_dim.7), calls=%async_computation.1 | async-start | bytes 16384 | tf_op jit(solution)/shard_map/all_to_all | solution.py:19
  140.7 12.5 %all-to-all-start.1 = ((f32[8,1,1]{2,1,0:T(1,128)}), f32[8,1,1]{2,1,0:T(1,128)S(1)}, u32[]{:S(2)}, u32[]{:S(2)}) async-start(f32[8,1,1]{2,1,0:T(1,128)} %broadcast_in_dim.8), calls=%async_computation.2 | async-start | bytes 8192 | tf_op jit(solution)/shard_map/all_to_all | solution.py:19
Sparse Core Ops, SparseCore 0:
  50.2 50.0 reduce-scatter.4
  102.8 22.0 reduce-scatter.6
where the time goes:
time: 163 us
  waiting for transfers between devices  83.3 us (51%)
  matrix products  26.1 us (16%)
  local copies, waits for them, and re-layouts  22.3 us (14%)
  between operations  15.4 us (9%)
  starting transfers between devices  12.8 us (8%)
  other arithmetic  3.18 us (2%)
    reduce_scatter x1, waiting for transfers between devices, summed_rows(): shard = lax.psum_scatter(shard, axis, scatter_dimension=dim, tiled=True)  50.2 us
    dot_general x1, matrix products, local(): partial_value = jnp.dot(masked, operand, preferred_element_type=jnp.float32)  26.1 us
    unnamed x3, waiting for transfers between devices  22.3 us
    unnamed x5, local copies, waits for them, and re-layouts  15.6 us
    all_to_all x2, starting transfers between devices, copy_for_each(): lax.all_to_all(jnp.broadcast_to(shard[None], (size, *shard.shape)), axis,...  12.7 us
    all_to_all x2, waiting for transfers between devices, copy_for_each(): lax.all_to_all(jnp.broadcast_to(shard[None], (size, *shard.shape)), axis,...  10.8 us
    mul x1, local copies, waits for them, and re-layouts, local(): adjacency.reshape(tiles_rows, TILE, tiles_cols, TILE) * keep_tile  3.82 us
  transfers between devices with their start and end apart: 4, of which 4 were waited for; matrix products, arithmetic and copies ran while one was open for 0% of the time, Pallas kernels for 0%

commit v1 on v0

v1 whole, which is shorter than its diff:
```python
import jax
import jax.numpy as jnp
from jax import lax
from jax.experimental import pallas as pl
from jax.experimental.pallas import tpu as pltpu
from jax.sharding import Mesh
from jax.sharding import PartitionSpec as P

TILE = 256
COL = ("col_0", "col_1")
ALL = ("row", "col_0", "col_1")
ROWS, DEPTH, COLS, LANES = 1024, 4096, 2048, 128
HALF = ROWS // 2
GROUP = 4 * LANES
KB = 512
F32, BF16 = jnp.float32, jnp.bfloat16
VMEM_LIMIT = 24 * 1024 * 1024


def column_block(pos, first, second):
    core, y, z = pos[0], pos[1], pos[2]
    by_y = core == 0
    dy = jnp.where(by_y, first, second)
    dz = jnp.where(by_y, second, first)
    return ((y + dy) & 3) * 4 + ((z + dz) & 3)


def moved(x, first, second):
    pairs = []
    for dev in range(128):
        row, y, z = dev // 16, dev // 4 % 4, dev % 4
        dy, dz = (first, second) if row % 2 == 0 else (second, first)
        pairs.append((dev, row * 16 + (y + dy) % 4 * 4 + (z + dz) % 4))
    return lax.ppermute(x, ALL, pairs)


def far_kernel(pos, mask, a, b0, b1, b2, b3, masked, out_a, out_b, acc):
    k = pl.program_id(0)
    per = KB // TILE
    rows = []
    for i in range(ROWS // TILE):
        tiles = []
        for j in range(per):
            keep = mask[i, k * per + j].astype(F32)
            tile = a[i * TILE:(i + 1) * TILE, j * TILE:(j + 1) * TILE]
            tiles.append(tile * jnp.full((TILE, TILE), keep, F32).astype(BF16))
        rows.append(jnp.concatenate(tiles, axis=1))
    kept = jnp.concatenate(rows, axis=0)
    masked[:, pl.ds(pl.multiple_of(k * KB, KB), KB)] = kept
    b = jnp.concatenate([b0[...], b1[...], b2[...], b3[...]], axis=1)
    part = jnp.dot(kept, b, preferred_element_type=F32)

    @pl.when(k == 0)
    def _():
        acc[...] = part

    @pl.when(jnp.logical_and(k > 0, k < DEPTH // KB - 1))
    def _():
        acc[...] += part

    @pl.when(k == DEPTH // KB - 1)
    def _():
        out_a[...] = (acc[:HALF] + part[:HALF]).astype(BF16)
        out_b[...] = (acc[HALF:] + part[HALF:]).astype(BF16)


def far_block(pos, mask, adjacency, operand):
    def b_spec(j):
        return pl.BlockSpec((KB, LANES), lambda k, pos: (k, column_block(pos, 2, j)))

    whole = pl.BlockSpec(memory_space=pltpu.VMEM)
    return pl.pallas_call(
        far_kernel,
        grid_spec=pltpu.PrefetchScalarGridSpec(
            num_scalar_prefetch=1,
            grid=(DEPTH // KB,),
            in_specs=[pl.BlockSpec(memory_space=pltpu.SMEM), pl.BlockSpec((ROWS, KB), lambda k, pos: (0, k))]
            + [b_spec(j) for j in range(4)],
            out_specs=[whole, whole, whole],
            scratch_shapes=[pltpu.VMEM((ROWS, GROUP), F32)],
        ),
        out_shape=[pltpu.VMEM((ROWS, DEPTH), BF16), pltpu.VMEM((HALF, GROUP), BF16), pltpu.VMEM((HALF, GROUP), BF16)],
        compiler_params=pltpu.CompilerParams(vmem_limit_bytes=VMEM_LIMIT),
        cost_estimate=pl.CostEstimate(flops=2 * ROWS * DEPTH * GROUP, transcendentals=0, bytes_accessed=12 << 20),
        name="far_block",
    )(pos, mask, adjacency, operand, operand, operand, operand)


def near_kernel(starts, merge, pos, masked, b0, b1, *rest):
    outs = rest[-2:]
    s = pl.program_id(0)
    b = jnp.concatenate([b0[...], b1[...]], axis=1)
    for part in (0, 1):
        for side in (0, 1):
            @pl.when(s == 2 * part + side)
            def _():
                lanes = slice(side * 2 * LANES, (side + 1) * 2 * LANES)
                block = jnp.dot(masked[starts[part]:starts[part] + HALF], b, preferred_element_type=F32)
                if merge:
                    block = block + rest[part][:, lanes].astype(F32)
                outs[part][:, lanes] = block.astype(BF16)


def near_blocks(pos, masked, operand, starts, arrived=()):
    def b_spec(j):
        return pl.BlockSpec(
            (DEPTH, LANES), lambda s, pos: (0, column_block(pos, jnp.where(s < 2, 1, 3), 2 * (s & 1) + j))
        )

    whole = pl.BlockSpec(memory_space=pltpu.VMEM)
    in_vmem = [pltpu.with_memory_space_constraint(x, pltpu.VMEM) for x in (masked, *arrived)]
    return pl.pallas_call(
        lambda *refs: near_kernel(starts, bool(arrived), *refs),
        grid_spec=pltpu.PrefetchScalarGridSpec(
            num_scalar_prefetch=1,
            grid=(4,),
            in_specs=[whole, b_spec(0), b_spec(1)] + [whole] * len(arrived),
            out_specs=[whole, whole],
        ),
        out_shape=[pltpu.VMEM((HALF, GROUP), BF16)] * 2,
        compiler_params=pltpu.CompilerParams(vmem_limit_bytes=VMEM_LIMIT),
        cost_estimate=pl.CostEstimate(flops=2 * ROWS * DEPTH * GROUP, transcendentals=0, bytes_accessed=8 << 20),
        name="near_merged" if arrived else "near_direct",
    )(pos, in_vmem[0], operand, operand, *in_vmem[1:])


def own_kernel(pos, masked, b0, b1, out):
    s = pl.program_id(0)
    b = jnp.concatenate([b0[...], b1[...]], axis=1)
    for side in (0, 1):
        @pl.when(s == side)
        def _():
            lanes = slice(side * 2 * LANES, (side + 1) * 2 * LANES)
            out[:, lanes] = jnp.dot(masked[...], b, preferred_element_type=F32)


def own_block(pos, masked, operand):
    def b_spec(j):
        return pl.BlockSpec((DEPTH, LANES), lambda s, pos: (0, column_block(pos, 0, 2 * s + j)))

    whole = pl.BlockSpec(memory_space=pltpu.VMEM)
    return pl.pallas_call(
        own_kernel,
        grid_spec=pltpu.PrefetchScalarGridSpec(
            num_scalar_prefetch=1, grid=(2,), in_specs=[whole, b_spec(0), b_spec(1)], out_specs=whole
        ),
        out_shape=pltpu.VMEM((ROWS, GROUP), F32),
        compiler_params=pltpu.CompilerParams(vmem_limit_bytes=VMEM_LIMIT),
        cost_estimate=pl.CostEstimate(flops=2 * ROWS * DEPTH * GROUP, transcendentals=0, bytes_accessed=4 << 20),
        name="own_block",
    )(pos, pltpu.with_memory_space_constraint(masked, pltpu.VMEM), operand, operand)


def second_kernel(own, next_a, back_a, back_b, next_b, mine, one, two, three):
    for part, (x, y) in enumerate(((next_a, back_a), (back_b, next_b))):
        rows = slice(part * HALF, (part + 1) * HALF)
        for j, out in enumerate((mine, one, two, three)):
            lanes = slice(j * LANES, (j + 1) * LANES)
            total = own[rows, lanes] + x[:, lanes].astype(F32) + y[:, lanes].astype(F32)
            out[rows, :] = total.astype(out.dtype)


def second_blocks(own, *arrived):
    whole = pl.BlockSpec(memory_space=pltpu.VMEM)
    return pl.pallas_call(
        second_kernel,
        in_specs=[whole] * 5,
        out_specs=[whole] * 4,
        out_shape=[pltpu.VMEM((ROWS, LANES), F32)] + [pltpu.VMEM((ROWS, LANES), BF16)] * 3,
        compiler_params=pltpu.CompilerParams(vmem_limit_bytes=VMEM_LIMIT),
        name="second_blocks",
    )(*(pltpu.with_memory_space_constraint(x, pltpu.VMEM) for x in (own, *arrived)))


def lift_kernel(mine, one, two, three, current, reached, gains):
    lane = lax.broadcasted_iota(jnp.int32, (1, LANES), 1)
    row = jnp.zeros((1, LANES), F32)
    for i in range(ROWS // TILE):
        rows = slice(i * TILE, (i + 1) * TILE)
        logits = mine[rows] + one[rows].astype(F32) + two[rows].astype(F32) + three[rows].astype(F32)
        prior = current[rows].astype(F32)
        lifted = (1.0 - prior) * jax.nn.sigmoid(logits)
        reached[rows, :] = (prior + lifted).astype(BF16)
        total = jnp.sum(jnp.sum(lifted, axis=0, keepdims=True), axis=1, keepdims=True)
        row = row + jnp.where(lane == i, total, 0.0)
    gains[...] = jnp.broadcast_to(row / (TILE * COLS), gains.shape)


def lift(mine, one, two, three, current):
    whole = pl.BlockSpec(memory_space=pltpu.VMEM)
    return pl.pallas_call(
        lift_kernel,
        in_specs=[whole] * 5,
        out_specs=[whole] * 2,
        out_shape=[jax.ShapeDtypeStruct((ROWS, LANES), BF16), jax.ShapeDtypeStruct((128, LANES), F32)],
        compiler_params=pltpu.CompilerParams(vmem_limit_bytes=VMEM_LIMIT),
        name="lift",
    )(mine, one, two, three, current)


def local(adjacency, tile_mask, operand, current):
    row = lax.axis_index("row")
    pos = jnp.stack([row & 1, lax.axis_index("col_0"), lax.axis_index("col_1")]).astype(jnp.int32)
    masked, far_a, far_b = far_block(pos, tile_mask, adjacency, operand)
    in_b = moved(far_b, 1, 0)
    in_a = moved(far_a, -1, 0)
    next_a, back_b = near_blocks(pos, masked, operand, (0, HALF))
    next_a = moved(next_a, 1, 0)
    back_b = moved(back_b, -1, 0)
    own = own_block(pos, masked, operand)
    next_b, back_a = near_blocks(pos, masked, operand, (HALF, 0), (in_b, in_a))
    next_b = moved(next_b, 1, 0)
    back_a = moved(back_a, -1, 0)
    mine, one, two, three = second_blocks(own, next_a, back_a, back_b, next_b)
    two = moved(two, 0, 2)
    one = moved(one, 0, 1)
    three = moved(three, 0, -1)
    reached, gains = lift(mine, one, two, three, current)
    gains = lax.all_to_all(gains, ALL, 0, 0, tiled=True)[:, :4]
    sender = lax.broadcasted_iota(jnp.int32, (128, 4, 4), 0) // 16
    earlier = lax.broadcasted_iota(jnp.int32, (128, 4, 4), 1) <= lax.broadcasted_iota(jnp.int32, (128, 4, 4), 2)
    counted = (sender < row) | ((sender == row) & earlier)
    progress = jnp.sum(jnp.where(counted, gains[:, :, None], 0.0), axis=(0, 1))
    return (reached, progress)


def solution(mesh):
    torus = Mesh(mesh.devices.reshape(mesh.shape["row"], 4, 4), ALL)
    in_specs = (P("row", COL), P("row", COL), P(COL, None), P("row", COL))
    out_specs = (P("row", COL), P("row"))
    return jax.shard_map(local, mesh=torus, in_specs=in_specs, out_specs=out_specs, check_vma=False)
```

time: 163 us -> 88.5 us (0.54)
  waiting for transfers between devices: 83.3 us -> 16.6 us
  Pallas kernels: 0 us -> 35.8 us
  matrix products: 26.1 us -> 0 us
  between operations: 15.4 us -> 0.72 us
  local copies, waits for them, and re-layouts: 22.3 us -> 9.9 us
  starting transfers between devices: 12.8 us -> 24.3 us
  other arithmetic: 3.18 us -> 0.75 us
    reduce_scatter x1 -> x0, waiting for transfers between devices: 50.2 us -> none  [summed_rows(): shard = lax.psum_scatter(shard, axis, scatter_dimension=dim, tiled=True)]
    pallas_call x0 -> x6, Pallas kernels: none -> 35.8 us  [the longest x2 17.5 us: near_blocks(): pl.pallas_call(lambda *refs: near_kernel(starts, bool(arrived), *refs), g...]
    dot_general x1 -> x0, matrix products: 26.1 us -> none  [local(): partial_value = jnp.dot(masked, operand, preferred_element_type=jnp.float32)]
    unnamed x3 -> x0, waiting for transfers between devices: 22.3 us -> none
    ppermute x0 -> x9, starting transfers between devices: none -> 13.8 us  [moved(): return lax.ppermute(x, ALL, pairs)]
    ppermute x0 -> x9, waiting for transfers between devices: none -> 7.07 us  [moved(): return lax.ppermute(x, ALL, pairs)]
    unnamed x5 -> x8, local copies, waits for them, and re-layouts: 15.6 us -> 9.84 us
    mul x1 -> x0, local copies, waits for them, and re-layouts: 3.82 us -> none  [local(): adjacency.reshape(tiles_rows, TILE, tiles_cols, TILE) * keep_tile]
  transfers between devices with their start and end apart: 4 -> 10, of which waited for: 4 -> 5; matrix products, arithmetic and copies ran while one was open for 0% -> 0% of each run, Pallas kernels for 0% -> 27%
where the time goes in v1:
time: 88.5 us; the launch traced here: 88.1 us
  Pallas kernels  35.8 us (40%)
  starting transfers between devices  24.3 us (27%)
  waiting for transfers between devices  16.6 us (19%)
  local copies, waits for them, and re-layouts  9.9 us (11%)
    pallas_call x2, Pallas kernels, near_blocks(): pl.pallas_call(lambda *refs: near_kernel(starts, bool(arrived), *refs), g...  17.5 us
    ppermute x9, starting transfers between devices, moved(): return lax.ppermute(x, ALL, pairs)  13.8 us
    all_to_all x1, starting transfers between devices, local(): gains = lax.all_to_all(gains, ALL, 0, 0, tiled=True)[:, :4]  10.5 us
    pallas_call x1, Pallas kernels, far_block(): pl.pallas_call(far_kernel, grid_spec=pltpu.PrefetchScalarGridSpec(num_sca...  10.2 us
    unnamed x8, local copies, waits for them, and re-layouts  9.84 us
    all_to_all x1, waiting for transfers between devices, local(): gains = lax.all_to_all(gains, ALL, 0, 0, tiled=True)[:, :4]  9.57 us
    ppermute x9, waiting for transfers between devices, moved(): return lax.ppermute(x, ALL, pairs)  7.07 us
    pallas_call x1, Pallas kernels, own_block(): pl.pallas_call(own_kernel, grid_spec=pltpu.PrefetchScalarGridSpec(num_sca...  6.75 us
  transfers between devices with their start and end apart: 10, of which 5 were waited for; matrix products, arithmetic and copies ran while one was open for 0% of the time, Pallas kernels for 27%

profile of v1, /device:TPU:1, one launch (start us, length us, event | category | flops | bytes accessed | tf_op | source)
XLA Modules:
  0.0 88.1 jit_solution(4551622459194289490)
XLA Ops:
  0.6 0.1 pad_add_fusion.pos.refs_0_
  0.7 3.4 %copy-done.1 = bf16[1024,4096]{1,0:T(8,128)(2,1)S(1)} copy-done((bf16[1024,4096]{1,0:T(8,128)(2,1)S(1)}, bf16[1024,4096]{1,0:T(8,128)(2,1)}, u32[]{:S(2)}) %copy-start.1) | copy-done | bytes 8388632
  4.1 0.7 copy-done.3
  4.8 10.2 %far_block.1 = (bf16[1024,4096]{1,0:T(8,128)(2,1)S(1)}, bf16[512,512]{1,0:T(8,128)(2,1)S(1)}, bf16[512,512]{1,0:T(8,128)(2,1)S(1)}) custom-call(s32[3]{0:T(128)S(1)} %pad_add_fusion.pos.refs_0_, s32[4,16]{1,0:T(4,128)S(1)} %copy-done.3, bf16[1024,4096]{1,0:T(8,128)(2,1)S(1)} %copy-done.1, bf16[4096,2048]{1,0:T(8,128)(2,1)} %refs_3_.3, ...), custom_call_target="tpu_custom_call" | custom-call | flops 4294967296 | bytes 12582912 | tf_op jit(solution)/shard_map/far_block/pallas_call | solution.py:72
  15.0 2.5 %collective-permute-start.1 = (bf16[512,512]{1,0:T(8,128)(2,1)S(1)}, bf16[512,512]{1,0:T(8,128)(2,1)S(1)}, u32[]{:S(2)}, u32[]{:S(2)}) collective-permute-start(bf16[512,512]{1,0:T(8,128)(2,1)S(1)} %get-tuple-element.17), channel_id=1, source_target_pairs={{0,4},{1,5},{2,6},{3,7},{4,8},{5,9},{6,10},{7,11},{8,12},{9,13},{1... | collective-permute-start | bytes 1572872 | tf_op jit(solution)/shard_map/ppermute | solution.py:34
  17.6 2.2 %collective-permute-start.2 = (bf16[512,512]{1,0:T(8,128)(2,1)S(1)}, bf16[512,512]{1,0:T(8,128)(2,1)S(1)}, u32[]{:S(2)}, u32[]{:S(2)}) collective-permute-start(bf16[512,512]{1,0:T(8,128)(2,1)S(1)} %get-tuple-element.18), channel_id=1, source_target_pairs={{0,12},{1,13},{2,14},{3,15},{4,0},{5,1},{6,2},{7,3},{8,4},{9,5},{1... | collective-permute-start | bytes 1572872 | tf_op jit(solution)/shard_map/ppermute | solution.py:34
  19.8 5.8 %copy-done = bf16[4096,2048]{1,0:T(8,128)(2,1)S(1)} copy-done((bf16[4096,2048]{1,0:T(8,128)(2,1)S(1)}, bf16[4096,2048]{1,0:T(8,128)(2,1)}, u32[]{:S(2)}) %copy-start) | copy-done | bytes 16777240
  25.5 8.7 %near_direct.1 = (bf16[512,512]{1,0:T(8,128)(2,1)S(1)}, bf16[512,512]{1,0:T(8,128)(2,1)S(1)}) custom-call(s32[3]{0:T(128)S(1)} %pad_add_fusion.pos.refs_0_, bf16[1024,4096]{1,0:T(8,128)(2,1)S(1)} %get-tuple-element.15.masked.refs_1_, bf16[4096,2048]{1,0:T(8,128)(2,1)S(1)} %copy-done, bf16[4096,2048]{1,0:T(8,128)(2,1)S(1)} %copy-done), custom_call_target="tpu_custom_call" | custom-call | flops 4294967296 | bytes 8388608 | tf_op jit(solution)/shard_map/near_direct/pallas_call | solution.py:112
  34.3 0.1 collective-permute-start
  34.3 2.7 %collective-permute-start.4 = (bf16[512,512]{1,0:T(8,128)(2,1)S(1)}, bf16[512,512]{1,0:T(8,128)(2,1)S(1)}, u32[]{:S(2)}, u32[]{:S(2)}) collective-permute-start(bf16[512,512]{1,0:T(8,128)(2,1)S(1)} %get-tuple-element.20), channel_id=1, source_target_pairs={{0,12},{1,13},{2,14},{3,15},{4,0},{5,1},{6,2},{7,3},{8,4},{9,5},{1... | collective-permute-start | bytes 1572872 | tf_op jit(solution)/shard_map/ppermute | solution.py:34
  37.0 0.0 collective-permute-done.1.refs_4_
  37.0 0.0 collective-permute-done.2.refs_5_
  37.0 8.7 %near_merged.1 = (bf16[512,512]{1,0:T(8,128)(2,1)S(1)}, bf16[512,512]{1,0:T(8,128)(2,1)S(1)}) custom-call(s32[3]{0:T(128)S(1)} %pad_add_fusion.pos.refs_0_, bf16[1024,4096]{1,0:T(8,128)(2,1)S(1)} %get-tuple-element.15.masked.refs_1_, bf16[4096,2048]{1,0:T(8,128)(2,1)S(1)} %copy-done, bf16[4096,2048]{1,0:T(8,128)(2,1)S(1)} %copy-done, ...), custom_call_target="tpu_custom_call" | custom-call | flops 4294967296 | bytes 8388608 | tf_op jit(solution)/shard_map/near_merged/pallas_call | solution.py:112
  45.8 0.3 collective-permute-start.3
  46.0 1.3 %collective-permute-start.5 = (bf16[512,512]{1,0:T(8,128)(2,1)S(1)}, bf16[512,512]{1,0:T(8,128)(2,1)S(1)}, u32[]{:S(2)}, u32[]{:S(2)}) collective-permute-start(bf16[512,512]{1,0:T(8,128)(2,1)S(1)} %get-tuple-element.21), channel_id=1, source_target_pairs={{0,4},{1,5},{2,6},{3,7},{4,8},{5,9},{6,10},{7,11},{8,12},{9,13},{1... | collective-permute-start | bytes 1572872 | tf_op jit(solution)/shard_map/ppermute | solution.py:34
  47.3 6.8 %own_block.1.own = f32[1024,512]{1,0:T(8,128)S(1)} custom-call(s32[3]{0:T(128)S(1)} %pad_add_fusion.pos.refs_0_, bf16[1024,4096]{1,0:T(8,128)(2,1)S(1)} %get-tuple-element.15.masked.refs_1_, bf16[4096,2048]{1,0:T(8,128)(2,1)S(1)} %copy-done, bf16[4096,2048]{1,0:T(8,128)(2,1)S(1)} %copy-done), custom_call_target="tpu_custom_call" | custom-call | flops 4294967296 | bytes 4194304 | tf_op jit(solution)/shard_map/own_block/pallas_call | solution.py:142
  54.1 0.0 collective-permute-done.next_a
  54.1 0.0 collective-permute-done.4.back_b
  54.1 0.1 collective-permute-done.3.back_a
  54.2 1.5 %collective-permute-done.5.next_b = bf16[512,512]{1,0:T(8,128)(2,1)S(1)} collective-permute-done((bf16[512,512]{1,0:T(8,128)(2,1)S(1)}, bf16[512,512]{1,0:T(8,128)(2,1)S(1)}, u32[]{:S(2)}, u32[]{:S(2)}) %collective-permute-start.5) | collective-permute-done | bytes 524320 | tf_op jit(solution)/shard_map/ppermute | solution.py:34
  55.6 0.4 second_blocks.1
  56.0 1.1 %collective-permute-start.6 = (bf16[1024,128]{1,0:T(8,128)(2,1)S(1)}, bf16[1024,128]{1,0:T(8,128)(2,1)S(1)}, u32[]{:S(2)}, u32[]{:S(2)}) collective-permute-start(bf16[1024,128]{1,0:T(8,128)(2,1)S(1)} %get-tuple-element.23), channel_id=1, source_target_pairs={{0,1},{1,2},{2,3},{3,0},{4,5},{5,6},{6,7},{7,4},{8,9},{9,10},{10,1... | collective-permute-start | bytes 786440 | tf_op jit(solution)/shard_map/ppermute | solution.py:34
  57.1 2.6 %collective-permute-start.7 = (bf16[1024,128]{1,0:T(8,128)(2,1)S(1)}, bf16[1024,128]{1,0:T(8,128)(2,1)S(1)}, u32[]{:S(2)}, u32[]{:S(2)}) collective-permute-start(bf16[1024,128]{1,0:T(8,128)(2,1)S(1)} %get-tuple-element.24), channel_id=1, source_target_pairs={{0,2},{1,3},{2,0},{3,1},{4,6},{5,7},{6,4},{7,5},{8,10},{9,11},{10,... | collective-permute-start | bytes 786440 | tf_op jit(solution)/shard_map/ppermute | solution.py:34
  59.7 1.1 %collective-permute-start.8 = (bf16[1024,128]{1,0:T(8,128)(2,1)S(1)}, bf16[1024,128]{1,0:T(8,128)(2,1)S(1)}, u32[]{:S(2)}, u32[]{:S(2)}) collective-permute-start(bf16[1024,128]{1,0:T(8,128)(2,1)S(1)} %get-tuple-element.25), channel_id=1, source_target_pairs={{0,3},{1,0},{2,1},{3,2},{4,7},{5,4},{6,5},{7,6},{8,11},{9,8},{10,9... | collective-permute-start | bytes 786440 | tf_op jit(solution)/shard_map/ppermute | solution.py:34
  60.8 1.7 %collective-permute-done.6.one = bf16[1024,128]{1,0:T(8,128)(2,1)S(1)} collective-permute-done((bf16[1024,128]{1,0:T(8,128)(2,1)S(1)}, bf16[1024,128]{1,0:T(8,128)(2,1)S(1)}, u32[]{:S(2)}, u32[]{:S(2)}) %collective-permute-start.6) | collective-permute-done | bytes 262176 | tf_op jit(solution)/shard_map/ppermute | solution.py:34
  62.5 3.8 %collective-permute-done.7.two = bf16[1024,128]{1,0:T(8,128)(2,1)S(1)} collective-permute-done((bf16[1024,128]{1,0:T(8,128)(2,1)S(1)}, bf16[1024,128]{1,0:T(8,128)(2,1)S(1)}, u32[]{:S(2)}, u32[]{:S(2)}) %collective-permute-start.7) | collective-permute-done | bytes 262176 | tf_op jit(solution)/shard_map/ppermute | solution.py:34
  66.3 0.0 collective-permute-done.8.three
  66.3 1.0 %lift.1 = (bf16[1024,128]{1,0:T(8,128)(2,1)}, f32[128,128]{1,0:T(8,128)}) custom-call(f32[1024,128]{1,0:T(8,128)S(1)} %get-tuple-element.22.mine, bf16[1024,128]{1,0:T(8,128)(2,1)S(1)} %collective-permute-done.6.one, bf16[1024,128]{1,0:T(8,128)(2,1)S(1)} %collective-permute-done.7.two, bf16[1024,128]{1,0:T(8,128)(2,1)S(1)} %collective-permute-done.8.three, ...), custom_call_target="tpu_custom_call" | custom-call | tf_op jit(solution)/shard_map/lift/pallas_call | solution.py:191
  67.3 10.5 %all-to-all-start = ((f32[128,1,128]{2,1,0:T(1,128)}), f32[128,1,128]{2,1,0:T(1,128)S(1)}, u32[]{:S(2)}, u32[]{:S(2)}) async-start(f32[128,1,128]{2,1,0:T(1,128)} %bitcast.4), calls=%async_computation | async-start | bytes 131072 | tf_op jit(solution)/shard_map/all_to_all | solution.py:219
  77.8 9.6 %all-to-all-done = f32[128,1,128]{2,1,0:T(1,128)S(1)} async-done(((f32[128,1,128]{2,1,0:T(1,128)}), f32[128,1,128]{2,1,0:T(1,128)S(1)}, u32[]{:S(2)}, u32[]{:S(2)}) %all-to-all-start) | async-done | bytes 65568 | tf_op jit(solution)/shard_map/all_to_all | solution.py:219
  87.4 0.1 copy.8
  87.4 0.7 select_reduce_fusion
  (7 shorter events, 0.0 us)
Async XLA Ops:
  0.7 3.4 %copy-start.1 = (bf16[1024,4096]{1,0:T(8,128)(2,1)S(1)}, bf16[1024,4096]{1,0:T(8,128)(2,1)}, u32[]{:S(2)}) copy-start(bf16[1024,4096]{1,0:T(8,128)(2,1)} %a.1) | copy-start | bytes 25165828
  4.1 0.7 copy-start.3
  15.0 22.0 %collective-permute-start.1 = (bf16[512,512]{1,0:T(8,128)(2,1)S(1)}, bf16[512,512]{1,0:T(8,128)(2,1)S(1)}, u32[]{:S(2)}, u32[]{:S(2)}) collective-permute-start(bf16[512,512]{1,0:T(8,128)(2,1)S(1)} %get-tuple-element.17), channel_id=1, source_target_pairs={{0,4},{1,5},{2,6},{3,7},{4,8},{5,9},{6,10},{7,11},{8,12},{9,13},{1... | collective-permute-start | bytes 1572872 | tf_op jit(solution)/shard_map/ppermute | solution.py:34
  17.6 19.5 %collective-permute-start.2 = (bf16[512,512]{1,0:T(8,128)(2,1)S(1)}, bf16[512,512]{1,0:T(8,128)(2,1)S(1)}, u32[]{:S(2)}, u32[]{:S(2)}) collective-permute-start(bf16[512,512]{1,0:T(8,128)(2,1)S(1)} %get-tuple-element.18), channel_id=1, source_target_pairs={{0,12},{1,13},{2,14},{3,15},{4,0},{5,1},{6,2},{7,3},{8,4},{9,5},{1... | collective-permute-start | bytes 1572872 | tf_op jit(solution)/shard_map/ppermute | solution.py:34
  19.8 5.8 %copy-start = (bf16[4096,2048]{1,0:T(8,128)(2,1)S(1)}, bf16[4096,2048]{1,0:T(8,128)(2,1)}, u32[]{:S(2)}) copy-start(bf16[4096,2048]{1,0:T(8,128)(2,1)} %refs_3_.3) | copy-start | bytes 50331652
  34.3 19.8 %collective-permute-start = (bf16[512,512]{1,0:T(8,128)(2,1)S(1)}, bf16[512,512]{1,0:T(8,128)(2,1)S(1)}, u32[]{:S(2)}, u32[]{:S(2)}) collective-permute-start(bf16[512,512]{1,0:T(8,128)(2,1)S(1)} %get-tuple-element.16), channel_id=1, source_target_pairs={{0,4},{1,5},{2,6},{3,7},{4,8},{5,9},{6,10},{7,11},{8,12},{9,13},{1... | collective-permute-start | bytes 1572872 | tf_op jit(solution)/shard_map/ppermute | solution.py:34
  34.3 19.7 %collective-permute-start.4 = (bf16[512,512]{1,0:T(8,128)(2,1)S(1)}, bf16[512,512]{1,0:T(8,128)(2,1)S(1)}, u32[]{:S(2)}, u32[]{:S(2)}) collective-permute-start(bf16[512,512]{1,0:T(8,128)(2,1)S(1)} %get-tuple-element.20), channel_id=1, source_target_pairs={{0,12},{1,13},{2,14},{3,15},{4,0},{5,1},{6,2},{7,3},{8,4},{9,5},{1... | collective-permute-start | bytes 1572872 | tf_op jit(solution)/shard_map/ppermute | solution.py:34
  45.8 8.4 %collective-permute-start.3 = (bf16[512,512]{1,0:T(8,128)(2,1)S(1)}, bf16[512,512]{1,0:T(8,128)(2,1)S(1)}, u32[]{:S(2)}, u32[]{:S(2)}) collective-permute-start(bf16[512,512]{1,0:T(8,128)(2,1)S(1)} %get-tuple-element.19), channel_id=1, source_target_pairs={{0,12},{1,13},{2,14},{3,15},{4,0},{5,1},{6,2},{7,3},{8,4},{9,5},{1... | collective-permute-start | bytes 1572872 | tf_op jit(solution)/shard_map/ppermute | solution.py:34
  46.0 20.3 %copy-start.2 = (bf16[1024,128]{1,0:T(8,128)(2,1)S(1)}, bf16[1024,128]{1,0:T(8,128)(2,1)}, u32[]{:S(2)}) copy-start(bf16[1024,128]{1,0:T(8,128)(2,1)} %current.1) | copy-start | bytes 786436
  46.0 9.6 %collective-permute-start.5 = (bf16[512,512]{1,0:T(8,128)(2,1)S(1)}, bf16[512,512]{1,0:T(8,128)(2,1)S(1)}, u32[]{:S(2)}, u32[]{:S(2)}) collective-permute-start(bf16[512,512]{1,0:T(8,128)(2,1)S(1)} %get-tuple-element.21), channel_id=1, source_target_pairs={{0,4},{1,5},{2,6},{3,7},{4,8},{5,9},{6,10},{7,11},{8,12},{9,13},{1... | collective-permute-start | bytes 1572872 | tf_op jit(solution)/shard_map/ppermute | solution.py:34
  56.0 6.5 %collective-permute-start.6 = (bf16[1024,128]{1,0:T(8,128)(2,1)S(1)}, bf16[1024,128]{1,0:T(8,128)(2,1)S(1)}, u32[]{:S(2)}, u32[]{:S(2)}) collective-permute-start(bf16[1024,128]{1,0:T(8,128)(2,1)S(1)} %get-tuple-element.23), channel_id=1, source_target_pairs={{0,1},{1,2},{2,3},{3,0},{4,5},{5,6},{6,7},{7,4},{8,9},{9,10},{10,1... | collective-permute-start | bytes 786440 | tf_op jit(solution)/shard_map/ppermute | solution.py:34
  57.1 9.2 %collective-permute-start.7 = (bf16[1024,128]{1,0:T(8,128)(2,1)S(1)}, bf16[1024,128]{1,0:T(8,128)(2,1)S(1)}, u32[]{:S(2)}, u32[]{:S(2)}) collective-permute-start(bf16[1024,128]{1,0:T(8,128)(2,1)S(1)} %get-tuple-element.24), channel_id=1, source_target_pairs={{0,2},{1,3},{2,0},{3,1},{4,6},{5,7},{6,4},{7,5},{8,10},{9,11},{10,... | collective-permute-start | bytes 786440 | tf_op jit(solution)/shard_map/ppermute | solution.py:34
  59.7 6.6 %collective-permute-start.8 = (bf16[1024,128]{1,0:T(8,128)(2,1)S(1)}, bf16[1024,128]{1,0:T(8,128)(2,1)S(1)}, u32[]{:S(2)}, u32[]{:S(2)}) collective-permute-start(bf16[1024,128]{1,0:T(8,128)(2,1)S(1)} %get-tuple-element.25), channel_id=1, source_target_pairs={{0,3},{1,0},{2,1},{3,2},{4,7},{5,4},{6,5},{7,6},{8,11},{9,8},{10,9... | collective-permute-start | bytes 786440 | tf_op jit(solution)/shard_map/ppermute | solution.py:34
  67.3 20.1 %all-to-all-start = ((f32[128,1,128]{2,1,0:T(1,128)}), f32[128,1,128]{2,1,0:T(1,128)S(1)}, u32[]{:S(2)}, u32[]{:S(2)}) async-start(f32[128,1,128]{2,1,0:T(1,128)} %bitcast.4), calls=%async_computation | async-start | bytes 131072 | tf_op jit(solution)/shard_map/all_to_all | solution.py:219

commit v2 on v1

v2 whole, which is shorter than its diff:
```python
import jax
import jax.numpy as jnp
from jax import lax
from jax.experimental import pallas as pl
from jax.experimental.pallas import tpu as pltpu
from jax.sharding import Mesh
from jax.sharding import PartitionSpec as P

TILE = 256
COL = ("col_0", "col_1")
ALL = ("row", "col_0", "col_1")
ROWS, DEPTH, COLS, LANES = 1024, 4096, 2048, 128
GROUP = 4 * LANES
SIDE = 2 * LANES
STEPS = ((0, 512), (512, 512), (1024, 1024), (2048, 1024), (3072, 1024))
F32, BF16 = jnp.float32, jnp.bfloat16
VMEM_LIMIT = 16 * 1024 * 1024


def position():
    return lax.axis_index("row") & 1, lax.axis_index("col_0"), lax.axis_index("col_1")


def column_block(pos, first, second):
    core, y, z = pos
    dy = first + core * (second - first)
    dz = second + core * (first - second)
    return ((y + dy) & 3) * 4 + ((z + dz) & 3)


def moved(x, first, second):
    pairs = []
    for dev in range(128):
        row, y, z = dev // 16, dev // 4 % 4, dev % 4
        dy, dz = (first, second) if row % 2 == 0 else (second, first)
        pairs.append((dev, row * 16 + (y + dy) % 4 * 4 + (z + dz) % 4))
    return lax.ppermute(x, ALL, pairs)


def columns_in(operand, pos, blocks, depth, bbuf, sems):
    return [
        pltpu.make_async_copy(
            operand.at[pl.ds(*depth), pl.ds(pl.multiple_of(column_block(pos, *block) * LANES, LANES), LANES)],
            bbuf.at[pl.ds(*depth), pl.ds(j * LANES, LANES)],
            sems.at[j],
        )
        for j, block in enumerate(blocks)
    ]


FAR = ((2, 0), (2, 1), (2, 2), (2, 3))
DIRECT = ((1, 0), (1, 1), (3, 2), (3, 3))
MERGED = ((3, 0), (3, 1), (1, 2), (1, 3))
OWN = ((0, 0), (0, 1), (0, 2), (0, 3))


def far_kernel(mask_hbm, adjacency, operand, masked, out_a, out_b, ahead_0, ahead_1, bbuf, acc, mask, mask_sem, a_sems, b_sems, ahead_sems):
    mask_copy = pltpu.make_async_copy(mask_hbm, mask, mask_sem)
    mask_copy.start()
    pos = position()
    a_copies, b_copies = [], []
    for k, (start, size) in enumerate(STEPS):
        depth = pl.ds(start, size)
        a_copies.append(pltpu.make_async_copy(adjacency.at[:, depth], masked.at[:, depth], a_sems.at[k]))
        a_copies[k].start()
        b_copies.append(columns_in(operand, pos, FAR, (start, size), bbuf, b_sems.at[k]))
        for copy in b_copies[k]:
            copy.start()
    ahead_copies = columns_in(operand, pos, DIRECT, (0, DEPTH), ahead_0, ahead_sems.at[0])
    ahead_copies += columns_in(operand, pos, MERGED, (0, DEPTH), ahead_1, ahead_sems.at[1])
    mask_copy.wait()
    for k, (start, size) in enumerate(STEPS):
        a_copies[k].wait()
        for i in range(ROWS // TILE):
            for j in range(start // TILE, (start + size) // TILE):
                @pl.when(mask[i, j] == 0)
                def _():
                    masked[i * TILE:(i + 1) * TILE, j * TILE:(j + 1) * TILE] = jnp.zeros((TILE, TILE), BF16)
        for copy in b_copies[k]:
            copy.wait()
        if k == 2:
            for copy in ahead_copies:
                copy.start()
        depth = slice(start, start + size)
        for i in range(ROWS // TILE):
            rows = slice(i * TILE, (i + 1) * TILE)
            part = jnp.dot(masked[rows, depth], bbuf[depth, :], preferred_element_type=F32)
            if k == 0:
                acc[rows, :] = part
            elif k < len(STEPS) - 1:
                acc[rows, :] += part
            else:
                out_a[rows, :] = (acc[rows, :SIDE] + part[:, :SIDE]).astype(BF16)
                out_b[rows, :] = (acc[rows, SIDE:] + part[:, SIDE:]).astype(BF16)
    for copy in ahead_copies:
        copy.wait()


WHOLE = pl.BlockSpec(memory_space=pltpu.VMEM)
IN_HBM = pl.BlockSpec(memory_space=pltpu.HBM)
MM_FLOPS = 2 * ROWS * DEPTH * GROUP
COLUMNS = pltpu.VMEM((DEPTH, GROUP), BF16)


def pinned(space, *arrays):
    return [pltpu.with_memory_space_constraint(x, space) for x in arrays]


def far_block(tile_mask, adjacency, operand):
    return pl.pallas_call(
        far_kernel,
        in_specs=[IN_HBM] * 3,
        out_specs=[WHOLE] * 5,
        scratch_shapes=[
            COLUMNS,
            pltpu.VMEM((ROWS, GROUP), F32),
            pltpu.SMEM((ROWS // TILE, DEPTH // TILE), jnp.int32),
            pltpu.SemaphoreType.DMA,
            pltpu.SemaphoreType.DMA((len(STEPS),)),
            pltpu.SemaphoreType.DMA((len(STEPS), 4)),
            pltpu.SemaphoreType.DMA((2, 4)),
        ],
        out_shape=[pltpu.VMEM((ROWS, DEPTH), BF16)] + [pltpu.VMEM((ROWS, SIDE), BF16)] * 2 + [COLUMNS] * 2,
        compiler_params=pltpu.CompilerParams(vmem_limit_bytes=VMEM_LIMIT),
        cost_estimate=pl.CostEstimate(flops=MM_FLOPS, transcendentals=0, bytes_accessed=20 << 20),
        name="far_block",
    )(*pinned(pltpu.HBM, tile_mask, adjacency, operand))


def near_kernel(merge, masked, columns, *rest):
    arrived, outs = rest[:-2], rest[-2:]
    for i in range(ROWS // TILE):
        rows = slice(i * TILE, (i + 1) * TILE)
        both = jnp.dot(masked[rows], columns[...], preferred_element_type=F32)
        for part, out in enumerate(outs):
            block = both[:, part * SIDE:(part + 1) * SIDE]
            if merge:
                block = block + arrived[part][rows].astype(F32)
            out[rows, :] = block.astype(BF16)


def near_blocks(masked, columns, arrived=()):
    return pl.pallas_call(
        lambda *refs: near_kernel(bool(arrived), *refs),
        in_specs=[WHOLE] * (2 + len(arrived)),
        out_specs=[WHOLE] * 2,
        out_shape=[pltpu.VMEM((ROWS, SIDE), BF16)] * 2,
        compiler_params=pltpu.CompilerParams(vmem_limit_bytes=VMEM_LIMIT),
        cost_estimate=pl.CostEstimate(flops=MM_FLOPS, transcendentals=0, bytes_accessed=0),
        name="near_merged" if arrived else "near_direct",
    )(*pinned(pltpu.VMEM, masked, columns, *arrived))


def own_kernel(masked, operand, out, bbuf, sems):
    pos = position()
    copies = []
    for k, step in enumerate(STEPS):
        copies.append(columns_in(operand, pos, OWN, step, bbuf, sems.at[k]))
        for copy in copies[k]:
            copy.start()
    for k, (start, size) in enumerate(STEPS):
        for copy in copies[k]:
            copy.wait()
        depth = slice(start, start + size)
        block = jnp.dot(masked[:, depth], bbuf[depth, :], preferred_element_type=F32)
        if k == 0:
            out[...] = block
        else:
            out[...] += block


def own_block(masked, operand):
    return pl.pallas_call(
        own_kernel,
        in_specs=[WHOLE, IN_HBM],
        out_specs=WHOLE,
        scratch_shapes=[pltpu.VMEM((DEPTH, GROUP), BF16), pltpu.SemaphoreType.DMA((len(STEPS), 4))],
        out_shape=pltpu.VMEM((ROWS, GROUP), F32),
        compiler_params=pltpu.CompilerParams(vmem_limit_bytes=VMEM_LIMIT),
        cost_estimate=pl.CostEstimate(flops=MM_FLOPS, transcendentals=0, bytes_accessed=4 << 20),
        name="own_block",
    )(*pinned(pltpu.VMEM, masked), *pinned(pltpu.HBM, operand))


def second_kernel(own, next_a, back_a, back_b, next_b, mine, one, two, three):
    for j, out in enumerate((mine, one, two, three)):
        x, y = (next_a, back_a) if j < 2 else (back_b, next_b)
        side = slice(j % 2 * LANES, (j % 2 + 1) * LANES)
        total = own[:, j * LANES:(j + 1) * LANES] + x[:, side].astype(F32) + y[:, side].astype(F32)
        out[...] = total.astype(out.dtype)


def second_blocks(own, *arrived):
    return pl.pallas_call(
        second_kernel,
        in_specs=[WHOLE] * 5,
        out_specs=[WHOLE] * 4,
        out_shape=[pltpu.VMEM((ROWS, LANES), F32)] + [pltpu.VMEM((ROWS, LANES), BF16)] * 3,
        compiler_params=pltpu.CompilerParams(vmem_limit_bytes=VMEM_LIMIT),
        name="second_blocks",
    )(*pinned(pltpu.VMEM, own, *arrived))


def lift_kernel(mine, one, two, three, current, reached, gains):
    lane = lax.broadcasted_iota(jnp.int32, (1, LANES), 1)
    row = jnp.zeros((1, LANES), F32)
    for i in range(ROWS // TILE):
        rows = slice(i * TILE, (i + 1) * TILE)
        logits = mine[rows] + one[rows].astype(F32) + two[rows].astype(F32) + three[rows].astype(F32)
        prior = current[rows].astype(F32)
        lifted = (1.0 - prior) * jax.nn.sigmoid(logits)
        reached[rows, :] = (prior + lifted).astype(BF16)
        total = jnp.sum(jnp.sum(lifted, axis=0, keepdims=True), axis=1, keepdims=True)
        row = row + jnp.where(lane == i, total, 0.0)
    gains[...] = jnp.broadcast_to(row / (TILE * COLS), gains.shape)


def lift(mine, one, two, three, current):
    return pl.pallas_call(
        lift_kernel,
        in_specs=[WHOLE] * 5,
        out_specs=[WHOLE] * 2,
        out_shape=[jax.ShapeDtypeStruct((ROWS, LANES), BF16), jax.ShapeDtypeStruct((128, LANES), F32)],
        compiler_params=pltpu.CompilerParams(vmem_limit_bytes=VMEM_LIMIT),
        name="lift",
    )(mine, one, two, three, current)


def local(adjacency, tile_mask, operand, current):
    row = lax.axis_index("row")
    masked, far_a, far_b, columns, more_columns = far_block(tile_mask, adjacency, operand)
    in_b = moved(far_b, 1, 0)
    in_a = moved(far_a, -1, 0)
    next_a, back_b = near_blocks(masked, columns)
    next_a = moved(next_a, 1, 0)
    back_b = moved(back_b, -1, 0)
    back_a, next_b = near_blocks(masked, more_columns, (in_a, in_b))
    next_b = moved(next_b, 1, 0)
    back_a = moved(back_a, -1, 0)
    own = own_block(masked, operand)
    mine, one, two, three = second_blocks(own, next_a, back_a, back_b, next_b)
    two = moved(two, 0, 2)
    one = moved(one, 0, 1)
    three = moved(three, 0, -1)
    reached, gains = lift(mine, two, one, three, current)
    gains = lax.all_to_all(gains, ALL, 0, 0, tiled=True)[:, :4]
    sender = lax.broadcasted_iota(jnp.int32, (128, 4, 4), 0) // 16
    earlier = lax.broadcasted_iota(jnp.int32, (128, 4, 4), 1) <= lax.broadcasted_iota(jnp.int32, (128, 4, 4), 2)
    counted = (sender < row) | ((sender == row) & earlier)
    progress = jnp.sum(jnp.where(counted, gains[:, :, None], 0.0), axis=(0, 1))
    return (reached, progress)


def solution(mesh):
    torus = Mesh(mesh.devices.reshape(mesh.shape["row"], 4, 4), ALL)
    in_specs = (P("row", COL), P("row", COL), P(COL, None), P("row", COL))
    out_specs = (P("row", COL), P("row"))
    return jax.shard_map(local, mesh=torus, in_specs=in_specs, out_specs=out_specs, check_vma=False)
```

time: 88.5 us -> 72.7 us (0.82)
  Pallas kernels: 35.8 us -> 24.5 us
  local copies, waits for them, and re-layouts: 9.9 us -> 0.06 us
  starting transfers between devices: 24.3 us -> 27.9 us
  waiting for transfers between devices: 16.6 us -> 18.5 us
    pallas_call x6, Pallas kernels: 35.8 us -> 24.5 us  [the longest x2 8.96 us: near_blocks(): pl.pallas_call(lambda *refs: near_kernel(bool(arrived), *refs), in_specs=...]
    unnamed x8 -> x2, local copies, waits for them, and re-layouts: 9.84 us -> 0.01 us
    all_to_all x1, starting transfers between devices: 10.5 us -> 13.7 us  [local(): gains = lax.all_to_all(gains, ALL, 0, 0, tiled=True)[:, :4]]
    ppermute x9, waiting for transfers between devices: 7.07 us -> 8.89 us  [moved(): return lax.ppermute(x, ALL, pairs)]
  transfers between devices with their start and end apart: 10 -> 10, of which waited for: 5 -> 7; matrix products, arithmetic and copies ran while one was open for 0% -> 0% of each run, Pallas kernels for 27% -> 21%
where the time goes in v2:
time: 72.7 us; the launch traced here: 72.3 us
  starting transfers between devices  27.9 us (38%)
  Pallas kernels  24.5 us (34%)
  waiting for transfers between devices  18.5 us (25%)
  between operations  0.73 us (1%)
    ppermute x9, starting transfers between devices, moved(): return lax.ppermute(x, ALL, pairs)  14.1 us
    all_to_all x1, starting transfers between devices, local(): gains = lax.all_to_all(gains, ALL, 0, 0, tiled=True)[:, :4]  13.7 us
    all_to_all x1, waiting for transfers between devices, local(): gains = lax.all_to_all(gains, ALL, 0, 0, tiled=True)[:, :4]  9.57 us
    pallas_call x2, Pallas kernels, near_blocks(): pl.pallas_call(lambda *refs: near_kernel(bool(arrived), *refs), in_specs=...  8.96 us
    ppermute x9, waiting for transfers between devices, moved(): return lax.ppermute(x, ALL, pairs)  8.89 us
    pallas_call x1, Pallas kernels, far_block(): pl.pallas_call(far_kernel, in_specs=[IN_HBM] * 3, out_specs=[WHOLE] * 5,...  8.19 us
    pallas_call x1, Pallas kernels, own_block(): pl.pallas_call(own_kernel, in_specs=[WHOLE, IN_HBM], out_specs=WHOLE, scr...  5.98 us
  transfers between devices with their start and end apart: 10, of which 7 were waited for; matrix products, arithmetic and copies ran while one was open for 0% of the time, Pallas kernels for 21%

profile of v2, /device:TPU:1, one launch (start us, length us, event | category | flops | bytes accessed | tf_op | source)
XLA Modules:
  0.0 72.3 jit_solution(17086862824656968517)
XLA Ops:
  0.6 8.2 %far_block.1 = (bf16[1024,4096]{1,0:T(8,128)(2,1)S(1)}, bf16[1024,256]{1,0:T(8,128)(2,1)S(1)}, bf16[1024,256]{1,0:T(8,128)(2,1)S(1)}, bf16[4096,512]{1,0:T(8,128)(2,1)S(1)}, bf16[4096,512]{1,0:T(8,128)(2,1)S(1)}) custom-call(s32[4,16]{1,0:T(4,128)} %mask_hbm.1, bf16[1024,4096]{1,0:T(8,128)(2,1)} %adjacency.1, bf16[4096,2048]{1,0:T(8,128)(2,1)} %operand.3), custom_call_target="tpu_custom_call" | custom-call | flops 4294967296 | bytes 20971520 | tf_op jit(solution)/shard_map/far_block/pallas_call | solution.py:110
  8.8 4.4 %collective-permute-start.1 = (bf16[1024,256]{1,0:T(8,128)(2,1)S(1)}, bf16[1024,256]{1,0:T(8,128)(2,1)S(1)}, u32[]{:S(2)}, u32[]{:S(2)}) collective-permute-start(bf16[1024,256]{1,0:T(8,128)(2,1)S(1)} %get-tuple-element.21), channel_id=1, source_target_pairs={{0,12},{1,13},{2,14},{3,15},{4,0},{5,1},{6,2},{7,3},{8,4},{9,5},{1... | collective-permute-start | bytes 1572872 | tf_op jit(solution)/shard_map/ppermute | solution.py:37
  13.2 0.0 collective-permute-start.2
  13.2 4.5 %near_direct.1 = (bf16[1024,256]{1,0:T(8,128)(2,1)S(1)}, bf16[1024,256]{1,0:T(8,128)(2,1)S(1)}) custom-call(bf16[1024,4096]{1,0:T(8,128)(2,1)S(1)} %get-tuple-element.17.masked.refs_0_, bf16[4096,512]{1,0:T(8,128)(2,1)S(1)} %get-tuple-element.18.refs_1_), custom_call_target="tpu_custom_call" | custom-call | flops 4294967296 | tf_op jit(solution)/shard_map/near_direct/pallas_call | solution.py:143
  17.7 0.1 collective-permute-start
  17.8 2.7 %collective-permute-start.4 = (bf16[1024,256]{1,0:T(8,128)(2,1)S(1)}, bf16[1024,256]{1,0:T(8,128)(2,1)S(1)}, u32[]{:S(2)}, u32[]{:S(2)}) collective-permute-start(bf16[1024,256]{1,0:T(8,128)(2,1)S(1)} %get-tuple-element.24), channel_id=1, source_target_pairs={{0,12},{1,13},{2,14},{3,15},{4,0},{5,1},{6,2},{7,3},{8,4},{9,5},{1... | collective-permute-start | bytes 1572872 | tf_op jit(solution)/shard_map/ppermute | solution.py:37
  20.5 0.0 collective-permute-done.1.refs_2_
  20.5 2.2 %collective-permute-done.2.refs_3_ = bf16[1024,256]{1,0:T(8,128)(2,1)S(1)} collective-permute-done((bf16[1024,256]{1,0:T(8,128)(2,1)S(1)}, bf16[1024,256]{1,0:T(8,128)(2,1)S(1)}, u32[]{:S(2)}, u32[]{:S(2)}) %collective-permute-start.2) | collective-permute-done | bytes 524320 | tf_op jit(solution)/shard_map/ppermute | solution.py:37
  22.8 4.5 %near_merged.1 = (bf16[1024,256]{1,0:T(8,128)(2,1)S(1)}, bf16[1024,256]{1,0:T(8,128)(2,1)S(1)}) custom-call(bf16[1024,4096]{1,0:T(8,128)(2,1)S(1)} %get-tuple-element.17.masked.refs_0_, bf16[4096,512]{1,0:T(8,128)(2,1)S(1)} %get-tuple-element.20.refs_1_, bf16[1024,256]{1,0:T(8,128)(2,1)S(1)} %collective-permute-done.1.refs_2_, ...), custom_call_target="tpu_custom_call" | custom-call | flops 4294967296 | tf_op jit(solution)/shard_map/near_merged/pallas_call | solution.py:143
  27.2 0.1 collective-permute-start.3
  27.3 0.0 copy-start
  27.3 1.4 %collective-permute-start.5 = (bf16[1024,256]{1,0:T(8,128)(2,1)S(1)}, bf16[1024,256]{1,0:T(8,128)(2,1)S(1)}, u32[]{:S(2)}, u32[]{:S(2)}) collective-permute-start(bf16[1024,256]{1,0:T(8,128)(2,1)S(1)} %get-tuple-element.25), channel_id=1, source_target_pairs={{0,4},{1,5},{2,6},{3,7},{4,8},{5,9},{6,10},{7,11},{8,12},{9,13},{1... | collective-permute-start | bytes 1572872 | tf_op jit(solution)/shard_map/ppermute | solution.py:37
  28.8 6.0 %own_block.1.own = f32[1024,512]{1,0:T(8,128)S(1)} custom-call(bf16[1024,4096]{1,0:T(8,128)(2,1)S(1)} %get-tuple-element.17.masked.refs_0_, bf16[4096,2048]{1,0:T(8,128)(2,1)} %operand.3), custom_call_target="tpu_custom_call" | custom-call | flops 4294967296 | bytes 4194304 | tf_op jit(solution)/shard_map/own_block/pallas_call | solution.py:173
  34.8 0.0 collective-permute-done.next_a
  34.8 0.0 collective-permute-done.4.back_b
  34.8 0.8 %collective-permute-done.3.back_a = bf16[1024,256]{1,0:T(8,128)(2,1)S(1)} collective-permute-done((bf16[1024,256]{1,0:T(8,128)(2,1)S(1)}, bf16[1024,256]{1,0:T(8,128)(2,1)S(1)}, u32[]{:S(2)}, u32[]{:S(2)}) %collective-permute-start.3) | collective-permute-done | bytes 524320 | tf_op jit(solution)/shard_map/ppermute | solution.py:37
  35.6 1.5 %collective-permute-done.5.next_b = bf16[1024,256]{1,0:T(8,128)(2,1)S(1)} collective-permute-done((bf16[1024,256]{1,0:T(8,128)(2,1)S(1)}, bf16[1024,256]{1,0:T(8,128)(2,1)S(1)}, u32[]{:S(2)}, u32[]{:S(2)}) %collective-permute-start.5) | collective-permute-done | bytes 524320 | tf_op jit(solution)/shard_map/ppermute | solution.py:37
  37.1 0.4 second_blocks.1
  37.5 2.7 %collective-permute-start.6 = (bf16[1024,128]{1,0:T(8,128)(2,1)S(1)}, bf16[1024,128]{1,0:T(8,128)(2,1)S(1)}, u32[]{:S(2)}, u32[]{:S(2)}) collective-permute-start(bf16[1024,128]{1,0:T(8,128)(2,1)S(1)} %get-tuple-element.27), channel_id=1, source_target_pairs={{0,2},{1,3},{2,0},{3,1},{4,6},{5,7},{6,4},{7,5},{8,10},{9,11},{10,... | collective-permute-start | bytes 786440 | tf_op jit(solution)/shard_map/ppermute | solution.py:37
  40.2 0.5 collective-permute-start.7
  40.7 2.2 %collective-permute-start.8 = (bf16[1024,128]{1,0:T(8,128)(2,1)S(1)}, bf16[1024,128]{1,0:T(8,128)(2,1)S(1)}, u32[]{:S(2)}, u32[]{:S(2)}) collective-permute-start(bf16[1024,128]{1,0:T(8,128)(2,1)S(1)} %get-tuple-element.29), channel_id=1, source_target_pairs={{0,3},{1,0},{2,1},{3,2},{4,7},{5,4},{6,5},{7,6},{8,11},{9,8},{10,9... | collective-permute-start | bytes 786440 | tf_op jit(solution)/shard_map/ppermute | solution.py:37
  42.9 1.7 %collective-permute-done.6.one = bf16[1024,128]{1,0:T(8,128)(2,1)S(1)} collective-permute-done((bf16[1024,128]{1,0:T(8,128)(2,1)S(1)}, bf16[1024,128]{1,0:T(8,128)(2,1)S(1)}, u32[]{:S(2)}, u32[]{:S(2)}) %collective-permute-start.6) | collective-permute-done | bytes 262176 | tf_op jit(solution)/shard_map/ppermute | solution.py:37
  44.6 2.5 %collective-permute-done.7.two = bf16[1024,128]{1,0:T(8,128)(2,1)S(1)} collective-permute-done((bf16[1024,128]{1,0:T(8,128)(2,1)S(1)}, bf16[1024,128]{1,0:T(8,128)(2,1)S(1)}, u32[]{:S(2)}, u32[]{:S(2)}) %collective-permute-start.7) | collective-permute-done | bytes 262176 | tf_op jit(solution)/shard_map/ppermute | solution.py:37
  47.1 0.1 collective-permute-done.8.three
  47.3 0.0 copy-done
  47.3 1.0 %lift.1 = (bf16[1024,128]{1,0:T(8,128)(2,1)}, f32[128,128]{1,0:T(8,128)}) custom-call(f32[1024,128]{1,0:T(8,128)S(1)} %get-tuple-element.26.mine, bf16[1024,128]{1,0:T(8,128)(2,1)S(1)} %collective-permute-done.6.one, bf16[1024,128]{1,0:T(8,128)(2,1)S(1)} %collective-permute-done.7.two, bf16[1024,128]{1,0:T(8,128)(2,1)S(1)} %collective-permute-done.8.three, ...), custom_call_target="tpu_custom_call" | custom-call | tf_op jit(solution)/shard_map/lift/pallas_call | solution.py:219
  48.2 13.7 %all-to-all-start = ((f32[128,1,128]{2,1,0:T(1,128)}), f32[128,1,128]{2,1,0:T(1,128)S(1)}, u32[]{:S(2)}, u32[]{:S(2)}) async-start(f32[128,1,128]{2,1,0:T(1,128)} %bitcast.1), calls=%async_computation | async-start | bytes 131072 | tf_op jit(solution)/shard_map/all_to_all | solution.py:246
  62.0 9.6 %all-to-all-done = f32[128,1,128]{2,1,0:T(1,128)S(1)} async-done(((f32[128,1,128]{2,1,0:T(1,128)}), f32[128,1,128]{2,1,0:T(1,128)S(1)}, u32[]{:S(2)}, u32[]{:S(2)}) %all-to-all-start) | async-done | bytes 65568 | tf_op jit(solution)/shard_map/all_to_all | solution.py:246
  71.6 0.1 copy.8
  71.6 0.7 select_reduce_fusion
  (2 shorter events, 0.0 us)
Async XLA Ops:
  8.8 11.7 %collective-permute-start.1 = (bf16[1024,256]{1,0:T(8,128)(2,1)S(1)}, bf16[1024,256]{1,0:T(8,128)(2,1)S(1)}, u32[]{:S(2)}, u32[]{:S(2)}) collective-permute-start(bf16[1024,256]{1,0:T(8,128)(2,1)S(1)} %get-tuple-element.21), channel_id=1, source_target_pairs={{0,12},{1,13},{2,14},{3,15},{4,0},{5,1},{6,2},{7,3},{8,4},{9,5},{1... | collective-permute-start | bytes 1572872 | tf_op jit(solution)/shard_map/ppermute | solution.py:37
  13.2 9.5 %collective-permute-start.2 = (bf16[1024,256]{1,0:T(8,128)(2,1)S(1)}, bf16[1024,256]{1,0:T(8,128)(2,1)S(1)}, u32[]{:S(2)}, u32[]{:S(2)}) collective-permute-start(bf16[1024,256]{1,0:T(8,128)(2,1)S(1)} %get-tuple-element.22), channel_id=1, source_target_pairs={{0,4},{1,5},{2,6},{3,7},{4,8},{5,9},{6,10},{7,11},{8,12},{9,13},{1... | collective-permute-start | bytes 1572872 | tf_op jit(solution)/shard_map/ppermute | solution.py:37
  17.7 17.1 %collective-permute-start = (bf16[1024,256]{1,0:T(8,128)(2,1)S(1)}, bf16[1024,256]{1,0:T(8,128)(2,1)S(1)}, u32[]{:S(2)}, u32[]{:S(2)}) collective-permute-start(bf16[1024,256]{1,0:T(8,128)(2,1)S(1)} %get-tuple-element.19), channel_id=1, source_target_pairs={{0,4},{1,5},{2,6},{3,7},{4,8},{5,9},{6,10},{7,11},{8,12},{9,13},{1... | collective-permute-start | bytes 1572872 | tf_op jit(solution)/shard_map/ppermute | solution.py:37
  17.8 17.0 %collective-permute-start.4 = (bf16[1024,256]{1,0:T(8,128)(2,1)S(1)}, bf16[1024,256]{1,0:T(8,128)(2,1)S(1)}, u32[]{:S(2)}, u32[]{:S(2)}) collective-permute-start(bf16[1024,256]{1,0:T(8,128)(2,1)S(1)} %get-tuple-element.24), channel_id=1, source_target_pairs={{0,12},{1,13},{2,14},{3,15},{4,0},{5,1},{6,2},{7,3},{8,4},{9,5},{1... | collective-permute-start | bytes 1572872 | tf_op jit(solution)/shard_map/ppermute | solution.py:37
  27.2 8.4 %collective-permute-start.3 = (bf16[1024,256]{1,0:T(8,128)(2,1)S(1)}, bf16[1024,256]{1,0:T(8,128)(2,1)S(1)}, u32[]{:S(2)}, u32[]{:S(2)}) collective-permute-start(bf16[1024,256]{1,0:T(8,128)(2,1)S(1)} %get-tuple-element.23), channel_id=1, source_target_pairs={{0,12},{1,13},{2,14},{3,15},{4,0},{5,1},{6,2},{7,3},{8,4},{9,5},{1... | collective-permute-start | bytes 1572872 | tf_op jit(solution)/shard_map/ppermute | solution.py:37
  27.3 19.9 %copy-start = (bf16[1024,128]{1,0:T(8,128)(2,1)S(1)}, bf16[1024,128]{1,0:T(8,128)(2,1)}, u32[]{:S(2)}) copy-start(bf16[1024,128]{1,0:T(8,128)(2,1)} %current.1) | copy-start | bytes 786436
  27.3 9.8 %collective-permute-start.5 = (bf16[1024,256]{1,0:T(8,128)(2,1)S(1)}, bf16[1024,256]{1,0:T(8,128)(2,1)S(1)}, u32[]{:S(2)}, u32[]{:S(2)}) collective-permute-start(bf16[1024,256]{1,0:T(8,128)(2,1)S(1)} %get-tuple-element.25), channel_id=1, source_target_pairs={{0,4},{1,5},{2,6},{3,7},{4,8},{5,9},{6,10},{7,11},{8,12},{9,13},{1... | collective-permute-start | bytes 1572872 | tf_op jit(solution)/shard_map/ppermute | solution.py:37
  37.5 7.1 %collective-permute-start.6 = (bf16[1024,128]{1,0:T(8,128)(2,1)S(1)}, bf16[1024,128]{1,0:T(8,128)(2,1)S(1)}, u32[]{:S(2)}, u32[]{:S(2)}) collective-permute-start(bf16[1024,128]{1,0:T(8,128)(2,1)S(1)} %get-tuple-element.27), channel_id=1, source_target_pairs={{0,2},{1,3},{2,0},{3,1},{4,6},{5,7},{6,4},{7,5},{8,10},{9,11},{10,... | collective-permute-start | bytes 786440 | tf_op jit(solution)/shard_map/ppermute | solution.py:37
  40.2 6.9 %collective-permute-start.7 = (bf16[1024,128]{1,0:T(8,128)(2,1)S(1)}, bf16[1024,128]{1,0:T(8,128)(2,1)S(1)}, u32[]{:S(2)}, u32[]{:S(2)}) collective-permute-start(bf16[1024,128]{1,0:T(8,128)(2,1)S(1)} %get-tuple-element.28), channel_id=1, source_target_pairs={{0,1},{1,2},{2,3},{3,0},{4,5},{5,6},{6,7},{7,4},{8,9},{9,10},{10,1... | collective-permute-start | bytes 786440 | tf_op jit(solution)/shard_map/ppermute | solution.py:37
  40.7 6.6 %collective-permute-start.8 = (bf16[1024,128]{1,0:T(8,128)(2,1)S(1)}, bf16[1024,128]{1,0:T(8,128)(2,1)S(1)}, u32[]{:S(2)}, u32[]{:S(2)}) collective-permute-start(bf16[1024,128]{1,0:T(8,128)(2,1)S(1)} %get-tuple-element.29), channel_id=1, source_target_pairs={{0,3},{1,0},{2,1},{3,2},{4,7},{5,4},{6,5},{7,6},{8,11},{9,8},{10,9... | collective-permute-start | bytes 786440 | tf_op jit(solution)/shard_map/ppermute | solution.py:37
  48.2 23.3 %all-to-all-start = ((f32[128,1,128]{2,1,0:T(1,128)}), f32[128,1,128]{2,1,0:T(1,128)S(1)}, u32[]{:S(2)}, u32[]{:S(2)}) async-start(f32[128,1,128]{2,1,0:T(1,128)} %bitcast.1), calls=%async_computation | async-start | bytes 131072 | tf_op jit(solution)/shard_map/all_to_all | solution.py:246

commit v3 on v2

--- a/solution.py
+++ b/solution.py
@@ -48,10 +48,10 @@
     ]
 
 
-FAR = ((2, 0), (2, 1), (2, 2), (2, 3))
-DIRECT = ((1, 0), (1, 1), (3, 2), (3, 3))
-MERGED = ((3, 0), (3, 1), (1, 2), (1, 3))
-OWN = ((0, 0), (0, 1), (0, 2), (0, 3))
+FAR = ((2, 0), (2, 2), (2, 1), (2, 3))
+DIRECT = ((1, 0), (1, 2), (3, 1), (3, 3))
+MERGED = ((3, 0), (3, 2), (1, 1), (1, 3))
+OWN = ((0, 0), (0, 2), (0, 1), (0, 3))
 
 
 def far_kernel(mask_hbm, adjacency, operand, masked, out_a, out_b, ahead_0, ahead_1, bbuf, acc, mask, mask_sem, a_sems, b_sems, ahead_sems):
@@ -122,7 +122,7 @@
         ],
         out_shape=[pltpu.VMEM((ROWS, DEPTH), BF16)] + [pltpu.VMEM((ROWS, SIDE), BF16)] * 2 + [COLUMNS] * 2,
         compiler_params=pltpu.CompilerParams(vmem_limit_bytes=VMEM_LIMIT),
-        cost_estimate=pl.CostEstimate(flops=MM_FLOPS, transcendentals=0, bytes_accessed=20 << 20),
+        cost_estimate=pl.CostEstimate(flops=8 * MM_FLOPS, transcendentals=0, bytes_accessed=20 << 20),
         name="far_block",
     )(*pinned(pltpu.HBM, tile_mask, adjacency, operand))
 
@@ -146,7 +146,7 @@
         out_specs=[WHOLE] * 2,
         out_shape=[pltpu.VMEM((ROWS, SIDE), BF16)] * 2,
         compiler_params=pltpu.CompilerParams(vmem_limit_bytes=VMEM_LIMIT),
-        cost_estimate=pl.CostEstimate(flops=MM_FLOPS, transcendentals=0, bytes_accessed=0),
+        cost_estimate=pl.CostEstimate(flops=8 * MM_FLOPS, transcendentals=0, bytes_accessed=0),
         name="near_merged" if arrived else "near_direct",
     )(*pinned(pltpu.VMEM, masked, columns, *arrived))
 
@@ -177,27 +177,27 @@
         scratch_shapes=[pltpu.VMEM((DEPTH, GROUP), BF16), pltpu.SemaphoreType.DMA((len(STEPS), 4))],
         out_shape=pltpu.VMEM((ROWS, GROUP), F32),
         compiler_params=pltpu.CompilerParams(vmem_limit_bytes=VMEM_LIMIT),
-        cost_estimate=pl.CostEstimate(flops=MM_FLOPS, transcendentals=0, bytes_accessed=4 << 20),
+        cost_estimate=pl.CostEstimate(flops=8 * MM_FLOPS, transcendentals=0, bytes_accessed=4 << 20),
         name="own_block",
     )(*pinned(pltpu.VMEM, masked), *pinned(pltpu.HBM, operand))
 
 
-def second_kernel(own, next_a, back_a, back_b, next_b, mine, one, two, three):
-    for j, out in enumerate((mine, one, two, three)):
-        x, y = (next_a, back_a) if j < 2 else (back_b, next_b)
-        side = slice(j % 2 * LANES, (j % 2 + 1) * LANES)
-        total = own[:, j * LANES:(j + 1) * LANES] + x[:, side].astype(F32) + y[:, side].astype(F32)
-        out[...] = total.astype(out.dtype)
-
-
-def second_blocks(own, *arrived):
-    return pl.pallas_call(
-        second_kernel,
-        in_specs=[WHOLE] * 5,
-        out_specs=[WHOLE] * 4,
-        out_shape=[pltpu.VMEM((ROWS, LANES), F32)] + [pltpu.VMEM((ROWS, LANES), BF16)] * 3,
-        compiler_params=pltpu.CompilerParams(vmem_limit_bytes=VMEM_LIMIT),
-        name="second_blocks",
+def second_kernel(side, own, x, y, *outs):
+    for j, out in enumerate(outs):
+        lanes = slice(j * LANES, (j + 1) * LANES)
+        mine = own[:, side * SIDE + j * LANES:side * SIDE + (j + 1) * LANES]
+        out[...] = (mine + x[:, lanes].astype(F32) + y[:, lanes].astype(F32)).astype(out.dtype)
+
+
+def second_blocks(side, dtypes, own, *arrived):
+    return pl.pallas_call(
+        lambda *refs: second_kernel(side, *refs),
+        in_specs=[WHOLE] * 3,
+        out_specs=[WHOLE] * 2,
+        out_shape=[pltpu.VMEM((ROWS, LANES), dtype) for dtype in dtypes],
+        compiler_params=pltpu.CompilerParams(vmem_limit_bytes=VMEM_LIMIT),
+        cost_estimate=pl.CostEstimate(flops=2 * ROWS * SIDE, transcendentals=0, bytes_accessed=0),
+        name=f"second_blocks_{side}",
     )(*pinned(pltpu.VMEM, own, *arrived))
 
 
@@ -238,8 +238,10 @@
     next_b = moved(next_b, 1, 0)
     back_a = moved(back_a, -1, 0)
     own = own_block(masked, operand)
-    mine, one, two, three = second_blocks(own, next_a, back_a, back_b, next_b)
+    mine, two = second_blocks(0, (F32, BF16), own, next_a, back_a)
+    own, two = lax.optimization_barrier((own, two))
     two = moved(two, 0, 2)
+    one, three = second_blocks(1, (BF16, BF16), own, back_b, next_b)
     one = moved(one, 0, 1)
     three = moved(three, 0, -1)
     reached, gains = lift(mine, two, one, three, current)

time: 72.7 us -> 69.9 us (0.961)
  starting transfers between devices: 27.9 us -> 23.4 us
  waiting for transfers between devices: 18.5 us -> 20.5 us
    all_to_all x1, starting transfers between devices: 13.7 us -> 10.7 us  [local(): gains = lax.all_to_all(gains, ALL, 0, 0, tiled=True)[:, :4]]
    ppermute x9, waiting for transfers between devices: 8.89 us -> 10.9 us  [moved(): return lax.ppermute(x, ALL, pairs)]
    ppermute x9, starting transfers between devices: 14.1 us -> 12.7 us  [moved(): return lax.ppermute(x, ALL, pairs)]
  transfers between devices with their start and end apart: 10 -> 10, of which waited for: 7 -> 7; matrix products, arithmetic and copies ran while one was open for 0% -> 0% of each run, Pallas kernels for 21% -> 22%
where the time goes in v3:
time: 69.9 us
  Pallas kernels  24.5 us (35%)
  starting transfers between devices  23.4 us (33%)
  waiting for transfers between devices  20.5 us (29%)
  between operations  0.73 us (1%)
    ppermute x9, starting transfers between devices, moved(): return lax.ppermute(x, ALL, pairs)  12.7 us
    ppermute x9, waiting for transfers between devices, moved(): return lax.ppermute(x, ALL, pairs)  10.9 us
    all_to_all x1, starting transfers between devices, local(): gains = lax.all_to_all(gains, ALL, 0, 0, tiled=True)[:, :4]  10.7 us
    all_to_all x1, waiting for transfers between devices, local(): gains = lax.all_to_all(gains, ALL, 0, 0, tiled=True)[:, :4]  9.55 us
    pallas_call x2, Pallas kernels, near_blocks(): pl.pallas_call(lambda *refs: near_kernel(bool(arrived), *refs), in_specs=...  8.96 us
    pallas_call x1, Pallas kernels, far_block(): pl.pallas_call(far_kernel, in_specs=[IN_HBM] * 3, out_specs=[WHOLE] * 5,...  8.24 us
    pallas_call x1, Pallas kernels, own_block(): pl.pallas_call(own_kernel, in_specs=[WHOLE, IN_HBM], out_specs=WHOLE, scr...  5.97 us
  transfers between devices with their start and end apart: 10, of which 7 were waited for; matrix products, arithmetic and copies ran while one was open for 0% of the time, Pallas kernels for 22%

profile of v3, /device:TPU:1, one launch (start us, length us, event | category | flops | bytes accessed | tf_op | source)
XLA Modules:
  0.0 69.9 jit_solution(10230444686107286927)
XLA Ops:
  0.6 8.2 %far_block.1 = (bf16[1024,4096]{1,0:T(8,128)(2,1)S(1)}, bf16[1024,256]{1,0:T(8,128)(2,1)S(1)}, bf16[1024,256]{1,0:T(8,128)(2,1)S(1)}, bf16[4096,512]{1,0:T(8,128)(2,1)S(1)}, bf16[4096,512]{1,0:T(8,128)(2,1)S(1)}) custom-call(s32[4,16]{1,0:T(4,128)} %mask_hbm.1, bf16[1024,4096]{1,0:T(8,128)(2,1)} %adjacency.1, bf16[4096,2048]{1,0:T(8,128)(2,1)} %operand.3), custom_call_target="tpu_custom_call" | custom-call | flops 34359738368 | bytes 20971520 | tf_op jit(solution)/shard_map/far_block/pallas_call | solution.py:110
  8.9 4.5 %collective-permute-start.1 = (bf16[1024,256]{1,0:T(8,128)(2,1)S(1)}, bf16[1024,256]{1,0:T(8,128)(2,1)S(1)}, u32[]{:S(2)}, u32[]{:S(2)}) collective-permute-start(bf16[1024,256]{1,0:T(8,128)(2,1)S(1)} %get-tuple-element.23), channel_id=1, source_target_pairs={{0,12},{1,13},{2,14},{3,15},{4,0},{5,1},{6,2},{7,3},{8,4},{9,5},{1... | collective-permute-start | bytes 1572872 | tf_op jit(solution)/shard_map/ppermute | solution.py:37
  13.4 0.0 collective-permute-start.2
  13.4 4.5 %near_direct.1 = (bf16[1024,256]{1,0:T(8,128)(2,1)S(1)}, bf16[1024,256]{1,0:T(8,128)(2,1)S(1)}) custom-call(bf16[1024,4096]{1,0:T(8,128)(2,1)S(1)} %get-tuple-element.19.masked.refs_0_, bf16[4096,512]{1,0:T(8,128)(2,1)S(1)} %get-tuple-element.20.refs_1_), custom_call_target="tpu_custom_call" | custom-call | flops 34359738368 | tf_op jit(solution)/shard_map/near_direct/pallas_call | solution.py:143
  17.9 0.1 collective-permute-start
  18.0 2.7 %collective-permute-start.5 = (bf16[1024,256]{1,0:T(8,128)(2,1)S(1)}, bf16[1024,256]{1,0:T(8,128)(2,1)S(1)}, u32[]{:S(2)}, u32[]{:S(2)}) collective-permute-start(bf16[1024,256]{1,0:T(8,128)(2,1)S(1)} %get-tuple-element.30), channel_id=1, source_target_pairs={{0,12},{1,13},{2,14},{3,15},{4,0},{5,1},{6,2},{7,3},{8,4},{9,5},{1... | collective-permute-start | bytes 1572872 | tf_op jit(solution)/shard_map/ppermute | solution.py:37
  20.7 0.0 collective-permute-done.1.refs_2_
  20.7 2.2 %collective-permute-done.2.refs_3_ = bf16[1024,256]{1,0:T(8,128)(2,1)S(1)} collective-permute-done((bf16[1024,256]{1,0:T(8,128)(2,1)S(1)}, bf16[1024,256]{1,0:T(8,128)(2,1)S(1)}, u32[]{:S(2)}, u32[]{:S(2)}) %collective-permute-start.2) | collective-permute-done | bytes 524320 | tf_op jit(solution)/shard_map/ppermute | solution.py:37
  22.9 4.5 %near_merged.1 = (bf16[1024,256]{1,0:T(8,128)(2,1)S(1)}, bf16[1024,256]{1,0:T(8,128)(2,1)S(1)}) custom-call(bf16[1024,4096]{1,0:T(8,128)(2,1)S(1)} %get-tuple-element.19.masked.refs_0_, bf16[4096,512]{1,0:T(8,128)(2,1)S(1)} %get-tuple-element.22.refs_1_, bf16[1024,256]{1,0:T(8,128)(2,1)S(1)} %collective-permute-done.1.refs_2_, ...), custom_call_target="tpu_custom_call" | custom-call | flops 34359738368 | tf_op jit(solution)/shard_map/near_merged/pallas_call | solution.py:143
  27.4 0.1 collective-permute-start.3
  27.5 0.0 copy-start
  27.5 1.4 %collective-permute-start.6 = (bf16[1024,256]{1,0:T(8,128)(2,1)S(1)}, bf16[1024,256]{1,0:T(8,128)(2,1)S(1)}, u32[]{:S(2)}, u32[]{:S(2)}) collective-permute-start(bf16[1024,256]{1,0:T(8,128)(2,1)S(1)} %get-tuple-element.31), channel_id=1, source_target_pairs={{0,4},{1,5},{2,6},{3,7},{4,8},{5,9},{6,10},{7,11},{8,12},{9,13},{1... | collective-permute-start | bytes 1572872 | tf_op jit(solution)/shard_map/ppermute | solution.py:37
  28.9 6.0 %own_block.1.refs_0_ = f32[1024,512]{1,0:T(8,128)S(1)} custom-call(bf16[1024,4096]{1,0:T(8,128)(2,1)S(1)} %get-tuple-element.19.masked.refs_0_, bf16[4096,2048]{1,0:T(8,128)(2,1)} %operand.3), custom_call_target="tpu_custom_call" | custom-call | flops 34359738368 | bytes 4194304 | tf_op jit(solution)/shard_map/own_block/pallas_call | solution.py:173
  34.9 0.0 collective-permute-done.refs_1_
  34.9 0.9 %collective-permute-done.3.refs_2_ = bf16[1024,256]{1,0:T(8,128)(2,1)S(1)} collective-permute-done((bf16[1024,256]{1,0:T(8,128)(2,1)S(1)}, bf16[1024,256]{1,0:T(8,128)(2,1)S(1)}, u32[]{:S(2)}, u32[]{:S(2)}) %collective-permute-start.3) | collective-permute-done | bytes 524320 | tf_op jit(solution)/shard_map/ppermute | solution.py:37
  35.8 0.2 second_blocks_0.1
  36.0 0.0 collective-permute-done.5.refs_1_
  36.0 1.3 %collective-permute-done.6.refs_2_ = bf16[1024,256]{1,0:T(8,128)(2,1)S(1)} collective-permute-done((bf16[1024,256]{1,0:T(8,128)(2,1)S(1)}, bf16[1024,256]{1,0:T(8,128)(2,1)S(1)}, u32[]{:S(2)}, u32[]{:S(2)}) %collective-permute-start.6) | collective-permute-done | bytes 524320 | tf_op jit(solution)/shard_map/ppermute | solution.py:37
  37.3 0.2 second_blocks_1.1
  37.5 0.6 collective-permute-start.7
  38.1 2.2 %collective-permute-start.8 = (bf16[1024,128]{1,0:T(8,128)(2,1)S(1)}, bf16[1024,128]{1,0:T(8,128)(2,1)S(1)}, u32[]{:S(2)}, u32[]{:S(2)}) collective-permute-start(bf16[1024,128]{1,0:T(8,128)(2,1)S(1)} %get-tuple-element.33), channel_id=1, source_target_pairs={{0,3},{1,0},{2,1},{3,2},{4,7},{5,4},{6,5},{7,6},{8,11},{9,8},{10,9... | collective-permute-start | bytes 786440 | tf_op jit(solution)/shard_map/ppermute | solution.py:37
  40.3 1.1 %collective-permute-start.4 = (bf16[1024,128]{1,0:T(8,128)(2,1)S(1)}, bf16[1024,128]{1,0:T(8,128)(2,1)S(1)}, u32[]{:S(2)}, u32[]{:S(2)}) collective-permute-start(bf16[1024,128]{1,0:T(8,128)(2,1)S(1)} %get-tuple-element.28), channel_id=1, source_target_pairs={{0,2},{1,3},{2,0},{3,1},{4,6},{5,7},{6,4},{7,5},{8,10},{9,11},{10,... | collective-permute-start | bytes 786440 | tf_op jit(solution)/shard_map/ppermute | solution.py:37
  41.4 2.6 %collective-permute-done.7.two = bf16[1024,128]{1,0:T(8,128)(2,1)S(1)} collective-permute-done((bf16[1024,128]{1,0:T(8,128)(2,1)S(1)}, bf16[1024,128]{1,0:T(8,128)(2,1)S(1)}, u32[]{:S(2)}, u32[]{:S(2)}) %collective-permute-start.7) | collective-permute-done | bytes 262176 | tf_op jit(solution)/shard_map/ppermute | solution.py:37
  44.0 2.4 %collective-permute-done.8.three = bf16[1024,128]{1,0:T(8,128)(2,1)S(1)} collective-permute-done((bf16[1024,128]{1,0:T(8,128)(2,1)S(1)}, bf16[1024,128]{1,0:T(8,128)(2,1)S(1)}, u32[]{:S(2)}, u32[]{:S(2)}) %collective-permute-start.8) | collective-permute-done | bytes 262176 | tf_op jit(solution)/shard_map/ppermute | solution.py:37
  46.4 1.5 %collective-permute-done.4.one = bf16[1024,128]{1,0:T(8,128)(2,1)S(1)} collective-permute-done((bf16[1024,128]{1,0:T(8,128)(2,1)S(1)}, bf16[1024,128]{1,0:T(8,128)(2,1)S(1)}, u32[]{:S(2)}, u32[]{:S(2)}) %collective-permute-start.4) | collective-permute-done | bytes 262176 | tf_op jit(solution)/shard_map/ppermute | solution.py:37
  47.9 0.0 copy-done
  47.9 1.0 %lift.1 = (bf16[1024,128]{1,0:T(8,128)(2,1)}, f32[128,128]{1,0:T(8,128)}) custom-call(f32[1024,128]{1,0:T(8,128)S(1)} %get-tuple-element.26.mine, bf16[1024,128]{1,0:T(8,128)(2,1)S(1)} %collective-permute-done.4.one, bf16[1024,128]{1,0:T(8,128)(2,1)S(1)} %collective-permute-done.7.two, bf16[1024,128]{1,0:T(8,128)(2,1)S(1)} %collective-permute-done.8.three, ...), custom_call_target="tpu_custom_call" | custom-call | tf_op jit(solution)/shard_map/lift/pallas_call | solution.py:219
  48.9 10.7 %all-to-all-start = ((f32[128,1,128]{2,1,0:T(1,128)}), f32[128,1,128]{2,1,0:T(1,128)S(1)}, u32[]{:S(2)}, u32[]{:S(2)}) async-start(f32[128,1,128]{2,1,0:T(1,128)} %bitcast.1), calls=%async_computation | async-start | bytes 131072 | tf_op jit(solution)/shard_map/all_to_all | solution.py:248
  59.6 9.5 %all-to-all-done = f32[128,1,128]{2,1,0:T(1,128)S(1)} async-done(((f32[128,1,128]{2,1,0:T(1,128)}), f32[128,1,128]{2,1,0:T(1,128)S(1)}, u32[]{:S(2)}, u32[]{:S(2)}) %all-to-all-start) | async-done | bytes 65568 | tf_op jit(solution)/shard_map/all_to_all | solution.py:248
  69.2 0.1 copy.8
  69.3 0.7 select_reduce_fusion
  (2 shorter events, 0.0 us)
Async XLA Ops:
  8.9 11.8 %collective-permute-start.1 = (bf16[1024,256]{1,0:T(8,128)(2,1)S(1)}, bf16[1024,256]{1,0:T(8,128)(2,1)S(1)}, u32[]{:S(2)}, u32[]{:S(2)}) collective-permute-start(bf16[1024,256]{1,0:T(8,128)(2,1)S(1)} %get-tuple-element.23), channel_id=1, source_target_pairs={{0,12},{1,13},{2,14},{3,15},{4,0},{5,1},{6,2},{7,3},{8,4},{9,5},{1... | collective-permute-start | bytes 1572872 | tf_op jit(solution)/shard_map/ppermute | solution.py:37
  13.4 9.5 %collective-permute-start.2 = (bf16[1024,256]{1,0:T(8,128)(2,1)S(1)}, bf16[1024,256]{1,0:T(8,128)(2,1)S(1)}, u32[]{:S(2)}, u32[]{:S(2)}) collective-permute-start(bf16[1024,256]{1,0:T(8,128)(2,1)S(1)} %get-tuple-element.24), channel_id=1, source_target_pairs={{0,4},{1,5},{2,6},{3,7},{4,8},{5,9},{6,10},{7,11},{8,12},{9,13},{1... | collective-permute-start | bytes 1572872 | tf_op jit(solution)/shard_map/ppermute | solution.py:37
  17.9 17.1 %collective-permute-start = (bf16[1024,256]{1,0:T(8,128)(2,1)S(1)}, bf16[1024,256]{1,0:T(8,128)(2,1)S(1)}, u32[]{:S(2)}, u32[]{:S(2)}) collective-permute-start(bf16[1024,256]{1,0:T(8,128)(2,1)S(1)} %get-tuple-element.21), channel_id=1, source_target_pairs={{0,4},{1,5},{2,6},{3,7},{4,8},{5,9},{6,10},{7,11},{8,12},{9,13},{1... | collective-permute-start | bytes 1572872 | tf_op jit(solution)/shard_map/ppermute | solution.py:37
  18.0 18.1 %collective-permute-start.5 = (bf16[1024,256]{1,0:T(8,128)(2,1)S(1)}, bf16[1024,256]{1,0:T(8,128)(2,1)S(1)}, u32[]{:S(2)}, u32[]{:S(2)}) collective-permute-start(bf16[1024,256]{1,0:T(8,128)(2,1)S(1)} %get-tuple-element.30), channel_id=1, source_target_pairs={{0,12},{1,13},{2,14},{3,15},{4,0},{5,1},{6,2},{7,3},{8,4},{9,5},{1... | collective-permute-start | bytes 1572872 | tf_op jit(solution)/shard_map/ppermute | solution.py:37
  27.4 8.4 %collective-permute-start.3 = (bf16[1024,256]{1,0:T(8,128)(2,1)S(1)}, bf16[1024,256]{1,0:T(8,128)(2,1)S(1)}, u32[]{:S(2)}, u32[]{:S(2)}) collective-permute-start(bf16[1024,256]{1,0:T(8,128)(2,1)S(1)} %get-tuple-element.25), channel_id=1, source_target_pairs={{0,12},{1,13},{2,14},{3,15},{4,0},{5,1},{6,2},{7,3},{8,4},{9,5},{1... | collective-permute-start | bytes 1572872 | tf_op jit(solution)/shard_map/ppermute | solution.py:37
  27.5 20.4 %copy-start = (bf16[1024,128]{1,0:T(8,128)(2,1)S(1)}, bf16[1024,128]{1,0:T(8,128)(2,1)}, u32[]{:S(2)}) copy-start(bf16[1024,128]{1,0:T(8,128)(2,1)} %current.1) | copy-start | bytes 786436
  27.5 9.8 %collective-permute-start.6 = (bf16[1024,256]{1,0:T(8,128)(2,1)S(1)}, bf16[1024,256]{1,0:T(8,128)(2,1)S(1)}, u32[]{:S(2)}, u32[]{:S(2)}) collective-permute-start(bf16[1024,256]{1,0:T(8,128)(2,1)S(1)} %get-tuple-element.31), channel_id=1, source_target_pairs={{0,4},{1,5},{2,6},{3,7},{4,8},{5,9},{6,10},{7,11},{8,12},{9,13},{1... | collective-permute-start | bytes 1572872 | tf_op jit(solution)/shard_map/ppermute | solution.py:37
  37.5 6.5 %collective-permute-start.7 = (bf16[1024,128]{1,0:T(8,128)(2,1)S(1)}, bf16[1024,128]{1,0:T(8,128)(2,1)S(1)}, u32[]{:S(2)}, u32[]{:S(2)}) collective-permute-start(bf16[1024,128]{1,0:T(8,128)(2,1)S(1)} %get-tuple-element.32), channel_id=1, source_target_pairs={{0,1},{1,2},{2,3},{3,0},{4,5},{5,6},{6,7},{7,4},{8,9},{9,10},{10,1... | collective-permute-start | bytes 786440 | tf_op jit(solution)/shard_map/ppermute | solution.py:37
  38.1 8.3 %collective-permute-start.8 = (bf16[1024,128]{1,0:T(8,128)(2,1)S(1)}, bf16[1024,128]{1,0:T(8,128)(2,1)S(1)}, u32[]{:S(2)}, u32[]{:S(2)}) collective-permute-start(bf16[1024,128]{1,0:T(8,128)(2,1)S(1)} %get-tuple-element.33), channel_id=1, source_target_pairs={{0,3},{1,0},{2,1},{3,2},{4,7},{5,4},{6,5},{7,6},{8,11},{9,8},{10,9... | collective-permute-start | bytes 786440 | tf_op jit(solution)/shard_map/ppermute | solution.py:37
  40.3 7.7 %collective-permute-start.4 = (bf16[1024,128]{1,0:T(8,128)(2,1)S(1)}, bf16[1024,128]{1,0:T(8,128)(2,1)S(1)}, u32[]{:S(2)}, u32[]{:S(2)}) collective-permute-start(bf16[1024,128]{1,0:T(8,128)(2,1)S(1)} %get-tuple-element.28), channel_id=1, source_target_pairs={{0,2},{1,3},{2,0},{3,1},{4,6},{5,7},{6,4},{7,5},{8,10},{9,11},{10,... | collective-permute-start | bytes 786440 | tf_op jit(solution)/shard_map/ppermute | solution.py:37
  48.9 20.3 %all-to-all-start = ((f32[128,1,128]{2,1,0:T(1,128)}), f32[128,1,128]{2,1,0:T(1,128)S(1)}, u32[]{:S(2)}, u32[]{:S(2)}) async-start(f32[128,1,128]{2,1,0:T(1,128)} %bitcast.1), calls=%async_computation | async-start | bytes 131072 | tf_op jit(solution)/shard_map/all_to_all | solution.py:248

commit v4 on v3

--- a/solution.py
+++ b/solution.py
@@ -182,7 +182,10 @@
     )(*pinned(pltpu.VMEM, masked), *pinned(pltpu.HBM, operand))
 
 
-def second_kernel(side, own, x, y, *outs):
+def second_kernel(side, own, x, y, *rest):
+    outs = rest[:2] if side == 0 else rest[-2:]
+    if side == 0:
+        rest[2][...] = own[:8, :LANES]
     for j, out in enumerate(outs):
         lanes = slice(j * LANES, (j + 1) * LANES)
         mine = own[:, side * SIDE + j * LANES:side * SIDE + (j + 1) * LANES]
@@ -190,11 +193,12 @@
 
 
 def second_blocks(side, dtypes, own, *arrived):
+    shapes = [(ROWS, LANES), (ROWS, LANES), (8, LANES)]
     return pl.pallas_call(
         lambda *refs: second_kernel(side, *refs),
-        in_specs=[WHOLE] * 3,
-        out_specs=[WHOLE] * 2,
-        out_shape=[pltpu.VMEM((ROWS, LANES), dtype) for dtype in dtypes],
+        in_specs=[WHOLE] * (1 + len(arrived)),
+        out_specs=[WHOLE] * len(dtypes),
+        out_shape=[pltpu.VMEM(shape, dtype) for shape, dtype in zip(shapes, dtypes)],
         compiler_params=pltpu.CompilerParams(vmem_limit_bytes=VMEM_LIMIT),
         cost_estimate=pl.CostEstimate(flops=2 * ROWS * SIDE, transcendentals=0, bytes_accessed=0),
         name=f"second_blocks_{side}",
@@ -203,7 +207,8 @@
 
 def lift_kernel(mine, one, two, three, current, reached, gains):
     lane = lax.broadcasted_iota(jnp.int32, (1, LANES), 1)
-    row = jnp.zeros((1, LANES), F32)
+    running = jnp.zeros((1, LANES), F32)
+    whole = jnp.zeros((1, LANES), F32)
     for i in range(ROWS // TILE):
         rows = slice(i * TILE, (i + 1) * TILE)
         logits = mine[rows] + one[rows].astype(F32) + two[rows].astype(F32) + three[rows].astype(F32)
@@ -211,8 +216,12 @@
         lifted = (1.0 - prior) * jax.nn.sigmoid(logits)
         reached[rows, :] = (prior + lifted).astype(BF16)
         total = jnp.sum(jnp.sum(lifted, axis=0, keepdims=True), axis=1, keepdims=True)
-        row = row + jnp.where(lane == i, total, 0.0)
-    gains[...] = jnp.broadcast_to(row / (TILE * COLS), gains.shape)
+        running = running + jnp.where(lane >= i, total, 0.0)
+        whole = whole + total
+    mine_row = lax.axis_index("row")
+    goes_to = lax.broadcasted_iota(jnp.int32, gains.shape, 0) // 16
+    sums = jnp.where(goes_to == mine_row, running, jnp.where(goes_to > mine_row, whole, 0.0))
+    gains[...] = sums / (TILE * COLS)
 
 
 def lift(mine, one, two, three, current):
@@ -227,7 +236,6 @@
 
 
 def local(adjacency, tile_mask, operand, current):
-    row = lax.axis_index("row")
     masked, far_a, far_b, columns, more_columns = far_block(tile_mask, adjacency, operand)
     in_b = moved(far_b, 1, 0)
     in_a = moved(far_a, -1, 0)
@@ -238,18 +246,14 @@
     next_b = moved(next_b, 1, 0)
     back_a = moved(back_a, -1, 0)
     own = own_block(masked, operand)
-    mine, two = second_blocks(0, (F32, BF16), own, next_a, back_a)
-    own, two = lax.optimization_barrier((own, two))
+    mine, two, token = second_blocks(0, (F32, BF16, F32), own, next_a, back_a)
+    token = lax.ppermute(token, ALL, [(dev, dev ^ 16) for dev in range(128)])
     two = moved(two, 0, 2)
-    one, three = second_blocks(1, (BF16, BF16), own, back_b, next_b)
+    one, three = second_blocks(1, (BF16, BF16), own, back_b, next_b, token)
     one = moved(one, 0, 1)
     three = moved(three, 0, -1)
     reached, gains = lift(mine, two, one, three, current)
-    gains = lax.all_to_all(gains, ALL, 0, 0, tiled=True)[:, :4]
-    sender = lax.broadcasted_iota(jnp.int32, (128, 4, 4), 0) // 16
-    earlier = lax.broadcasted_iota(jnp.int32, (128, 4, 4), 1) <= lax.broadcasted_iota(jnp.int32, (128, 4, 4), 2)
-    counted = (sender < row) | ((sender == row) & earlier)
-    progress = jnp.sum(jnp.where(counted, gains[:, :, None], 0.0), axis=(0, 1))
+    progress = jnp.sum(lax.all_to_all(gains, ALL, 0, 0, tiled=True)[:, :ROWS // TILE], axis=0)
     return (reached, progress)
 
 

time: 69.9 us -> 67.7 us (0.969)
  blocking collectives: 0 us -> 18.3 us
  waiting for transfers between devices: 20.5 us -> 9.06 us
  starting transfers between devices: 23.4 us -> 14.7 us
    all_to_all x0 -> x1, blocking collectives: none -> 18.3 us  [local(): lax.all_to_all(gains, ALL, 0, 0, tiled=True)[:, :ROWS // TILE]]
    all_to_all x1 -> x0, starting transfers between devices: 10.7 us -> none  [local(): gains = lax.all_to_all(gains, ALL, 0, 0, tiled=True)[:, :4]]
    all_to_all x1 -> x0, waiting for transfers between devices: 9.55 us -> none  [local(): gains = lax.all_to_all(gains, ALL, 0, 0, tiled=True)[:, :4]]
    ppermute x9, waiting for transfers between devices: 10.9 us -> 9.06 us  [moved(): return lax.ppermute(x, ALL, pairs)]
    ppermute x0 -> x1, starting transfers between devices: none -> 1.75 us  [local(): token = lax.ppermute(token, ALL, [(dev, dev ^ 16) for dev in range(128)])]
  transfers between devices with their start and end apart: 10 -> 10, of which waited for: 7 -> 4; matrix products, arithmetic and copies ran while one was open for 0% -> 0% of each run, Pallas kernels for 22% -> 23%
where the time goes in v4:
time: 67.7 us; the launch traced here: 67.5 us
  Pallas kernels  24.2 us (36%)
  blocking collectives  18.3 us (27%)
  starting transfers between devices  14.7 us (22%)
  waiting for transfers between devices  9.06 us (13%)
  between operations  0.71 us (1%)
    all_to_all x1, blocking collectives, local(): lax.all_to_all(gains, ALL, 0, 0, tiled=True)[:, :ROWS // TILE]  18.3 us
    ppermute x9, starting transfers between devices, moved(): return lax.ppermute(x, ALL, pairs)  13 us
    ppermute x9, waiting for transfers between devices, moved(): return lax.ppermute(x, ALL, pairs)  9.06 us
    pallas_call x2, Pallas kernels, near_blocks(): pl.pallas_call(lambda *refs: near_kernel(bool(arrived), *refs), in_specs=...  8.96 us
    pallas_call x1, Pallas kernels, far_block(): pl.pallas_call(far_kernel, in_specs=[IN_HBM] * 3, out_specs=[WHOLE] * 5,...  7.91 us
    pallas_call x1, Pallas kernels, own_block(): pl.pallas_call(own_kernel, in_specs=[WHOLE, IN_HBM], out_specs=WHOLE, scr...  5.96 us
    ppermute x1, starting transfers between devices, local(): token = lax.ppermute(token, ALL, [(dev, dev ^ 16) for dev in range(128)])  1.75 us
  transfers between devices with their start and end apart: 10, of which 4 were waited for; matrix products, arithmetic and copies ran while one was open for 0% of the time, Pallas kernels for 23%

profile of v4, /device:TPU:1, one launch (start us, length us, event | category | flops | bytes accessed | tf_op | source)
XLA Modules:
  0.0 67.5 jit_solution(15181687949924582795)
XLA Ops:
  0.6 7.9 %far_block.1 = (bf16[1024,4096]{1,0:T(8,128)(2,1)S(1)}, bf16[1024,256]{1,0:T(8,128)(2,1)S(1)}, bf16[1024,256]{1,0:T(8,128)(2,1)S(1)}, bf16[4096,512]{1,0:T(8,128)(2,1)S(1)}, bf16[4096,512]{1,0:T(8,128)(2,1)S(1)}) custom-call(s32[4,16]{1,0:T(4,128)} %mask_hbm.1, bf16[1024,4096]{1,0:T(8,128)(2,1)} %adjacency.1, bf16[4096,2048]{1,0:T(8,128)(2,1)} %operand.3), custom_call_target="tpu_custom_call" | custom-call | flops 34359738368 | bytes 20971520 | tf_op jit(solution)/shard_map/far_block/pallas_call | solution.py:110
  8.5 5.0 %collective-permute-start.1 = (bf16[1024,256]{1,0:T(8,128)(2,1)S(1)}, bf16[1024,256]{1,0:T(8,128)(2,1)S(1)}, u32[]{:S(2)}, u32[]{:S(2)}) collective-permute-start(bf16[1024,256]{1,0:T(8,128)(2,1)S(1)} %get-tuple-element.22), channel_id=1, source_target_pairs={{0,12},{1,13},{2,14},{3,15},{4,0},{5,1},{6,2},{7,3},{8,4},{9,5},{1... | collective-permute-start | bytes 1572872 | tf_op jit(solution)/shard_map/ppermute | solution.py:37
  13.5 0.0 collective-permute-start.2
  13.5 4.5 %near_direct.1 = (bf16[1024,256]{1,0:T(8,128)(2,1)S(1)}, bf16[1024,256]{1,0:T(8,128)(2,1)S(1)}) custom-call(bf16[1024,4096]{1,0:T(8,128)(2,1)S(1)} %get-tuple-element.18.masked.refs_0_, bf16[4096,512]{1,0:T(8,128)(2,1)S(1)} %get-tuple-element.19.refs_1_), custom_call_target="tpu_custom_call" | custom-call | flops 34359738368 | tf_op jit(solution)/shard_map/near_direct/pallas_call | solution.py:143
  18.0 0.1 collective-permute-start
  18.1 2.7 %collective-permute-start.5 = (bf16[1024,256]{1,0:T(8,128)(2,1)S(1)}, bf16[1024,256]{1,0:T(8,128)(2,1)S(1)}, u32[]{:S(2)}, u32[]{:S(2)}) collective-permute-start(bf16[1024,256]{1,0:T(8,128)(2,1)S(1)} %get-tuple-element.27), channel_id=1, source_target_pairs={{0,12},{1,13},{2,14},{3,15},{4,0},{5,1},{6,2},{7,3},{8,4},{9,5},{1... | collective-permute-start | bytes 1572872 | tf_op jit(solution)/shard_map/ppermute | solution.py:37
  20.8 0.0 collective-permute-done.1.refs_2_
  20.8 2.2 %collective-permute-done.2.refs_3_ = bf16[1024,256]{1,0:T(8,128)(2,1)S(1)} collective-permute-done((bf16[1024,256]{1,0:T(8,128)(2,1)S(1)}, bf16[1024,256]{1,0:T(8,128)(2,1)S(1)}, u32[]{:S(2)}, u32[]{:S(2)}) %collective-permute-start.2) | collective-permute-done | bytes 524320 | tf_op jit(solution)/shard_map/ppermute | solution.py:37
  23.0 4.5 %near_merged.1 = (bf16[1024,256]{1,0:T(8,128)(2,1)S(1)}, bf16[1024,256]{1,0:T(8,128)(2,1)S(1)}) custom-call(bf16[1024,4096]{1,0:T(8,128)(2,1)S(1)} %get-tuple-element.18.masked.refs_0_, bf16[4096,512]{1,0:T(8,128)(2,1)S(1)} %get-tuple-element.21.refs_1_, bf16[1024,256]{1,0:T(8,128)(2,1)S(1)} %collective-permute-done.1.refs_2_, ...), custom_call_target="tpu_custom_call" | custom-call | flops 34359738368 | tf_op jit(solution)/shard_map/near_merged/pallas_call | solution.py:143
  27.5 0.1 collective-permute-start.3
  27.6 0.0 copy-start
  27.6 1.4 %collective-permute-start.6 = (bf16[1024,256]{1,0:T(8,128)(2,1)S(1)}, bf16[1024,256]{1,0:T(8,128)(2,1)S(1)}, u32[]{:S(2)}, u32[]{:S(2)}) collective-permute-start(bf16[1024,256]{1,0:T(8,128)(2,1)S(1)} %get-tuple-element.28), channel_id=1, source_target_pairs={{0,4},{1,5},{2,6},{3,7},{4,8},{5,9},{6,10},{7,11},{8,12},{9,13},{1... | collective-permute-start | bytes 1572872 | tf_op jit(solution)/shard_map/ppermute | solution.py:37
  29.1 6.0 %own_block.1.refs_0_ = f32[1024,512]{1,0:T(8,128)S(1)} custom-call(bf16[1024,4096]{1,0:T(8,128)(2,1)S(1)} %get-tuple-element.18.masked.refs_0_, bf16[4096,2048]{1,0:T(8,128)(2,1)} %operand.3), custom_call_target="tpu_custom_call" | custom-call | flops 34359738368 | bytes 4194304 | tf_op jit(solution)/shard_map/own_block/pallas_call | solution.py:173
  35.0 0.0 collective-permute-done.refs_1_
  35.0 0.9 %collective-permute-done.3.refs_2_ = bf16[1024,256]{1,0:T(8,128)(2,1)S(1)} collective-permute-done((bf16[1024,256]{1,0:T(8,128)(2,1)S(1)}, bf16[1024,256]{1,0:T(8,128)(2,1)S(1)}, u32[]{:S(2)}, u32[]{:S(2)}) %collective-permute-start.3) | collective-permute-done | bytes 524320 | tf_op jit(solution)/shard_map/ppermute | solution.py:37
  35.9 0.2 second_blocks_0.1
  36.1 1.7 %collective-permute-start.7 = (f32[8,128]{1,0:T(8,128)S(1)}, f32[8,128]{1,0:T(8,128)S(1)}, u32[]{:S(2)}, u32[]{:S(2)}) collective-permute-start(f32[8,128]{1,0:T(8,128)S(1)} %get-tuple-element.29), channel_id=1, source_target_pairs={{0,16},{1,17},{2,18},{3,19},{4,20},{5,21},{6,22},{7,23},{8,24},{9,... | collective-permute-start | bytes 12296 | tf_op jit(solution)/shard_map/ppermute | solution.py:250
  37.9 0.9 %collective-permute-start.4 = (bf16[1024,128]{1,0:T(8,128)(2,1)S(1)}, bf16[1024,128]{1,0:T(8,128)(2,1)S(1)}, u32[]{:S(2)}, u32[]{:S(2)}) collective-permute-start(bf16[1024,128]{1,0:T(8,128)(2,1)S(1)} %get-tuple-element.26), channel_id=1, source_target_pairs={{0,2},{1,3},{2,0},{3,1},{4,6},{5,7},{6,4},{7,5},{8,10},{9,11},{10,... | collective-permute-start | bytes 786440 | tf_op jit(solution)/shard_map/ppermute | solution.py:37
  38.8 0.0 collective-permute-done.5.refs_1_
  38.8 0.0 collective-permute-done.6.refs_2_
  38.8 0.0 collective-permute-done.7.refs_3_
  38.8 0.2 second_blocks_1.1
  39.0 0.7 collective-permute-start.8
  39.7 2.1 %collective-permute-start.9 = (bf16[1024,128]{1,0:T(8,128)(2,1)S(1)}, bf16[1024,128]{1,0:T(8,128)(2,1)S(1)}, u32[]{:S(2)}, u32[]{:S(2)}) collective-permute-start(bf16[1024,128]{1,0:T(8,128)(2,1)S(1)} %get-tuple-element.31), channel_id=1, source_target_pairs={{0,3},{1,0},{2,1},{3,2},{4,7},{5,4},{6,5},{7,6},{8,11},{9,8},{10,9... | collective-permute-start | bytes 786440 | tf_op jit(solution)/shard_map/ppermute | solution.py:37
  41.8 3.2 %collective-permute-done.4.one = bf16[1024,128]{1,0:T(8,128)(2,1)S(1)} collective-permute-done((bf16[1024,128]{1,0:T(8,128)(2,1)S(1)}, bf16[1024,128]{1,0:T(8,128)(2,1)S(1)}, u32[]{:S(2)}, u32[]{:S(2)}) %collective-permute-start.4) | collective-permute-done | bytes 262176 | tf_op jit(solution)/shard_map/ppermute | solution.py:37
  44.9 2.8 %collective-permute-done.8.two = bf16[1024,128]{1,0:T(8,128)(2,1)S(1)} collective-permute-done((bf16[1024,128]{1,0:T(8,128)(2,1)S(1)}, bf16[1024,128]{1,0:T(8,128)(2,1)S(1)}, u32[]{:S(2)}, u32[]{:S(2)}) %collective-permute-start.8) | collective-permute-done | bytes 262176 | tf_op jit(solution)/shard_map/ppermute | solution.py:37
  47.7 0.0 collective-permute-done.9.three
  47.7 0.0 copy-done
  47.7 1.0 %lift.1 = (bf16[1024,128]{1,0:T(8,128)(2,1)}, f32[128,128]{1,0:T(8,128)S(1)}) custom-call(f32[1024,128]{1,0:T(8,128)S(1)} %get-tuple-element.25.mine, bf16[1024,128]{1,0:T(8,128)(2,1)S(1)} %collective-permute-done.4.one, bf16[1024,128]{1,0:T(8,128)(2,1)S(1)} %collective-permute-done.8.two, bf16[1024,128]{1,0:T(8,128)(2,1)S(1)} %collective-permute-done.9.three, ...), custom_call_target="tpu_custom_call" | custom-call | tf_op jit(solution)/shard_map/lift/pallas_call | solution.py:228
  48.7 18.3 %all_to_all.12 = f32[128,1,128]{2,1,0:T(1,128)S(1)} all-to-all(f32[128,1,128]{2,1,0:T(1,128)S(1)} %bitcast.4), channel_id=1, replica_groups=mesh['row'=8,'col_0'=4,'col_1'=4] {'row','col_0','col_1'}, dimensions={0} | all-to-all | bytes 131072 | tf_op jit(solution)/shard_map/all_to_all | solution.py:256
  67.0 0.5 slice_reduce_fusion
Async XLA Ops:
  8.5 12.3 %collective-permute-start.1 = (bf16[1024,256]{1,0:T(8,128)(2,1)S(1)}, bf16[1024,256]{1,0:T(8,128)(2,1)S(1)}, u32[]{:S(2)}, u32[]{:S(2)}) collective-permute-start(bf16[1024,256]{1,0:T(8,128)(2,1)S(1)} %get-tuple-element.22), channel_id=1, source_target_pairs={{0,12},{1,13},{2,14},{3,15},{4,0},{5,1},{6,2},{7,3},{8,4},{9,5},{1... | collective-permute-start | bytes 1572872 | tf_op jit(solution)/shard_map/ppermute | solution.py:37
  13.5 9.5 %collective-permute-start.2 = (bf16[1024,256]{1,0:T(8,128)(2,1)S(1)}, bf16[1024,256]{1,0:T(8,128)(2,1)S(1)}, u32[]{:S(2)}, u32[]{:S(2)}) collective-permute-start(bf16[1024,256]{1,0:T(8,128)(2,1)S(1)} %get-tuple-element.23), channel_id=1, source_target_pairs={{0,4},{1,5},{2,6},{3,7},{4,8},{5,9},{6,10},{7,11},{8,12},{9,13},{1... | collective-permute-start | bytes 1572872 | tf_op jit(solution)/shard_map/ppermute | solution.py:37
  18.0 17.0 %collective-permute-start = (bf16[1024,256]{1,0:T(8,128)(2,1)S(1)}, bf16[1024,256]{1,0:T(8,128)(2,1)S(1)}, u32[]{:S(2)}, u32[]{:S(2)}) collective-permute-start(bf16[1024,256]{1,0:T(8,128)(2,1)S(1)} %get-tuple-element.20), channel_id=1, source_target_pairs={{0,4},{1,5},{2,6},{3,7},{4,8},{5,9},{6,10},{7,11},{8,12},{9,13},{1... | collective-permute-start | bytes 1572872 | tf_op jit(solution)/shard_map/ppermute | solution.py:37
  18.1 20.7 %collective-permute-start.5 = (bf16[1024,256]{1,0:T(8,128)(2,1)S(1)}, bf16[1024,256]{1,0:T(8,128)(2,1)S(1)}, u32[]{:S(2)}, u32[]{:S(2)}) collective-permute-start(bf16[1024,256]{1,0:T(8,128)(2,1)S(1)} %get-tuple-element.27), channel_id=1, source_target_pairs={{0,12},{1,13},{2,14},{3,15},{4,0},{5,1},{6,2},{7,3},{8,4},{9,5},{1... | collective-permute-start | bytes 1572872 | tf_op jit(solution)/shard_map/ppermute | solution.py:37
  27.5 8.4 %collective-permute-start.3 = (bf16[1024,256]{1,0:T(8,128)(2,1)S(1)}, bf16[1024,256]{1,0:T(8,128)(2,1)S(1)}, u32[]{:S(2)}, u32[]{:S(2)}) collective-permute-start(bf16[1024,256]{1,0:T(8,128)(2,1)S(1)} %get-tuple-element.24), channel_id=1, source_target_pairs={{0,12},{1,13},{2,14},{3,15},{4,0},{5,1},{6,2},{7,3},{8,4},{9,5},{1... | collective-permute-start | bytes 1572872 | tf_op jit(solution)/shard_map/ppermute | solution.py:37
  27.6 20.1 %copy-start = (bf16[1024,128]{1,0:T(8,128)(2,1)S(1)}, bf16[1024,128]{1,0:T(8,128)(2,1)}, u32[]{:S(2)}) copy-start(bf16[1024,128]{1,0:T(8,128)(2,1)} %current.1) | copy-start | bytes 786436
  27.6 11.2 %collective-permute-start.6 = (bf16[1024,256]{1,0:T(8,128)(2,1)S(1)}, bf16[1024,256]{1,0:T(8,128)(2,1)S(1)}, u32[]{:S(2)}, u32[]{:S(2)}) collective-permute-start(bf16[1024,256]{1,0:T(8,128)(2,1)S(1)} %get-tuple-element.28), channel_id=1, source_target_pairs={{0,4},{1,5},{2,6},{3,7},{4,8},{5,9},{6,10},{7,11},{8,12},{9,13},{1... | collective-permute-start | bytes 1572872 | tf_op jit(solution)/shard_map/ppermute | solution.py:37
  36.1 2.7 %collective-permute-start.7 = (f32[8,128]{1,0:T(8,128)S(1)}, f32[8,128]{1,0:T(8,128)S(1)}, u32[]{:S(2)}, u32[]{:S(2)}) collective-permute-start(f32[8,128]{1,0:T(8,128)S(1)} %get-tuple-element.29), channel_id=1, source_target_pairs={{0,16},{1,17},{2,18},{3,19},{4,20},{5,21},{6,22},{7,23},{8,24},{9,... | collective-permute-start | bytes 12296 | tf_op jit(solution)/shard_map/ppermute | solution.py:250
  37.9 7.1 %collective-permute-start.4 = (bf16[1024,128]{1,0:T(8,128)(2,1)S(1)}, bf16[1024,128]{1,0:T(8,128)(2,1)S(1)}, u32[]{:S(2)}, u32[]{:S(2)}) collective-permute-start(bf16[1024,128]{1,0:T(8,128)(2,1)S(1)} %get-tuple-element.26), channel_id=1, source_target_pairs={{0,2},{1,3},{2,0},{3,1},{4,6},{5,7},{6,4},{7,5},{8,10},{9,11},{10,... | collective-permute-start | bytes 786440 | tf_op jit(solution)/shard_map/ppermute | solution.py:37
  39.0 8.7 %collective-permute-start.8 = (bf16[1024,128]{1,0:T(8,128)(2,1)S(1)}, bf16[1024,128]{1,0:T(8,128)(2,1)S(1)}, u32[]{:S(2)}, u32[]{:S(2)}) collective-permute-start(bf16[1024,128]{1,0:T(8,128)(2,1)S(1)} %get-tuple-element.30), channel_id=1, source_target_pairs={{0,1},{1,2},{2,3},{3,0},{4,5},{5,6},{6,7},{7,4},{8,9},{9,10},{10,1... | collective-permute-start | bytes 786440 | tf_op jit(solution)/shard_map/ppermute | solution.py:37
  39.7 8.0 %collective-permute-start.9 = (bf16[1024,128]{1,0:T(8,128)(2,1)S(1)}, bf16[1024,128]{1,0:T(8,128)(2,1)S(1)}, u32[]{:S(2)}, u32[]{:S(2)}) collective-permute-start(bf16[1024,128]{1,0:T(8,128)(2,1)S(1)} %get-tuple-element.31), channel_id=1, source_target_pairs={{0,3},{1,0},{2,1},{3,2},{4,7},{5,4},{6,5},{7,6},{8,11},{9,8},{10,9... | collective-permute-start | bytes 786440 | tf_op jit(solution)/shard_map/ppermute | solution.py:37

commit v5 on v4

--- a/solution.py
+++ b/solution.py
@@ -248,6 +248,7 @@
     own = own_block(masked, operand)
     mine, two, token = second_blocks(0, (F32, BF16, F32), own, next_a, back_a)
     token = lax.ppermute(token, ALL, [(dev, dev ^ 16) for dev in range(128)])
+    two, token = lax.optimization_barrier((two, token))
     two = moved(two, 0, 2)
     one, three = second_blocks(1, (BF16, BF16), own, back_b, next_b, token)
     one = moved(one, 0, 1)

time: 67.7 us -> 68.9 us (1.018)
    ppermute x1, waiting for transfers between devices: 0.01 us -> 0.82 us  [local(): token = lax.ppermute(token, ALL, [(dev, dev ^ 16) for dev in range(128)])]
  transfers between devices with their start and end apart: 10 -> 10, of which waited for: 4 -> 5; matrix products, arithmetic and copies ran while one was open for 0% -> 0% of each run, Pallas kernels for 23% -> 22%
where the time goes in v5:
time: 68.9 us; the launch traced here: 68.6 us
  Pallas kernels  24.3 us (35%)
  blocking collectives  18.6 us (27%)
  starting transfers between devices  14.7 us (21%)
  waiting for transfers between devices  9.74 us (14%)
  between operations  0.71 us (1%)
    all_to_all x1, blocking collectives, local(): lax.all_to_all(gains, ALL, 0, 0, tiled=True)[:, :ROWS // TILE]  18.6 us
    ppermute x9, starting transfers between devices, moved(): return lax.ppermute(x, ALL, pairs)  12.7 us
    pallas_call x2, Pallas kernels, near_blocks(): pl.pallas_call(lambda *refs: near_kernel(bool(arrived), *refs), in_specs=...  8.96 us
    ppermute x9, waiting for transfers between devices, moved(): return lax.ppermute(x, ALL, pairs)  8.92 us
    pallas_call x1, Pallas kernels, far_block(): pl.pallas_call(far_kernel, in_specs=[IN_HBM] * 3, out_specs=[WHOLE] * 5,...  7.99 us
    pallas_call x1, Pallas kernels, own_block(): pl.pallas_call(own_kernel, in_specs=[WHOLE, IN_HBM], out_specs=WHOLE, scr...  5.96 us
    ppermute x1, starting transfers between devices, local(): token = lax.ppermute(token, ALL, [(dev, dev ^ 16) for dev in range(128)])  1.97 us
  transfers between devices with their start and end apart: 10, of which 5 were waited for; matrix products, arithmetic and copies ran while one was open for 0% of the time, Pallas kernels for 22%

profile of v5, /device:TPU:1, one launch (start us, length us, event | category | flops | bytes accessed | tf_op | source)
XLA Modules:
  0.0 68.6 jit_solution(7712949415052713651)
XLA Ops:
  0.6 8.0 %far_block.1 = (bf16[1024,4096]{1,0:T(8,128)(2,1)S(1)}, bf16[1024,256]{1,0:T(8,128)(2,1)S(1)}, bf16[1024,256]{1,0:T(8,128)(2,1)S(1)}, bf16[4096,512]{1,0:T(8,128)(2,1)S(1)}, bf16[4096,512]{1,0:T(8,128)(2,1)S(1)}) custom-call(s32[4,16]{1,0:T(4,128)} %mask_hbm.1, bf16[1024,4096]{1,0:T(8,128)(2,1)} %adjacency.1, bf16[4096,2048]{1,0:T(8,128)(2,1)} %operand.3), custom_call_target="tpu_custom_call" | custom-call | flops 34359738368 | bytes 20971520 | tf_op jit(solution)/shard_map/far_block/pallas_call | solution.py:110
  8.6 4.6 %collective-permute-start.1 = (bf16[1024,256]{1,0:T(8,128)(2,1)S(1)}, bf16[1024,256]{1,0:T(8,128)(2,1)S(1)}, u32[]{:S(2)}, u32[]{:S(2)}) collective-permute-start(bf16[1024,256]{1,0:T(8,128)(2,1)S(1)} %get-tuple-element.24), channel_id=1, source_target_pairs={{0,12},{1,13},{2,14},{3,15},{4,0},{5,1},{6,2},{7,3},{8,4},{9,5},{1... | collective-permute-start | bytes 1572872 | tf_op jit(solution)/shard_map/ppermute | solution.py:37
  13.2 0.0 collective-permute-start.2
  13.2 4.5 %near_direct.1 = (bf16[1024,256]{1,0:T(8,128)(2,1)S(1)}, bf16[1024,256]{1,0:T(8,128)(2,1)S(1)}) custom-call(bf16[1024,4096]{1,0:T(8,128)(2,1)S(1)} %get-tuple-element.20.masked.refs_0_, bf16[4096,512]{1,0:T(8,128)(2,1)S(1)} %get-tuple-element.21.refs_1_), custom_call_target="tpu_custom_call" | custom-call | flops 34359738368 | tf_op jit(solution)/shard_map/near_direct/pallas_call | solution.py:143
  17.7 0.1 collective-permute-start
  17.8 2.7 %collective-permute-start.6 = (bf16[1024,256]{1,0:T(8,128)(2,1)S(1)}, bf16[1024,256]{1,0:T(8,128)(2,1)S(1)}, u32[]{:S(2)}, u32[]{:S(2)}) collective-permute-start(bf16[1024,256]{1,0:T(8,128)(2,1)S(1)} %get-tuple-element.31), channel_id=1, source_target_pairs={{0,12},{1,13},{2,14},{3,15},{4,0},{5,1},{6,2},{7,3},{8,4},{9,5},{1... | collective-permute-start | bytes 1572872 | tf_op jit(solution)/shard_map/ppermute | solution.py:37
  20.5 0.0 collective-permute-done.1.refs_2_
  20.5 2.2 %collective-permute-done.2.refs_3_ = bf16[1024,256]{1,0:T(8,128)(2,1)S(1)} collective-permute-done((bf16[1024,256]{1,0:T(8,128)(2,1)S(1)}, bf16[1024,256]{1,0:T(8,128)(2,1)S(1)}, u32[]{:S(2)}, u32[]{:S(2)}) %collective-permute-start.2) | collective-permute-done | bytes 524320 | tf_op jit(solution)/shard_map/ppermute | solution.py:37
  22.7 4.5 %near_merged.1 = (bf16[1024,256]{1,0:T(8,128)(2,1)S(1)}, bf16[1024,256]{1,0:T(8,128)(2,1)S(1)}) custom-call(bf16[1024,4096]{1,0:T(8,128)(2,1)S(1)} %get-tuple-element.20.masked.refs_0_, bf16[4096,512]{1,0:T(8,128)(2,1)S(1)} %get-tuple-element.23.refs_1_, bf16[1024,256]{1,0:T(8,128)(2,1)S(1)} %collective-permute-done.1.refs_2_, ...), custom_call_target="tpu_custom_call" | custom-call | flops 34359738368 | tf_op jit(solution)/shard_map/near_merged/pallas_call | solution.py:143
  27.2 0.1 collective-permute-start.3
  27.3 0.0 copy-start
  27.3 1.4 %collective-permute-start.7 = (bf16[1024,256]{1,0:T(8,128)(2,1)S(1)}, bf16[1024,256]{1,0:T(8,128)(2,1)S(1)}, u32[]{:S(2)}, u32[]{:S(2)}) collective-permute-start(bf16[1024,256]{1,0:T(8,128)(2,1)S(1)} %get-tuple-element.32), channel_id=1, source_target_pairs={{0,4},{1,5},{2,6},{3,7},{4,8},{5,9},{6,10},{7,11},{8,12},{9,13},{1... | collective-permute-start | bytes 1572872 | tf_op jit(solution)/shard_map/ppermute | solution.py:37
  28.8 6.0 %own_block.1.refs_0_ = f32[1024,512]{1,0:T(8,128)S(1)} custom-call(bf16[1024,4096]{1,0:T(8,128)(2,1)S(1)} %get-tuple-element.20.masked.refs_0_, bf16[4096,2048]{1,0:T(8,128)(2,1)} %operand.3), custom_call_target="tpu_custom_call" | custom-call | flops 34359738368 | bytes 4194304 | tf_op jit(solution)/shard_map/own_block/pallas_call | solution.py:173
  34.7 0.0 collective-permute-done.refs_1_
  34.7 0.9 %collective-permute-done.3.refs_2_ = bf16[1024,256]{1,0:T(8,128)(2,1)S(1)} collective-permute-done((bf16[1024,256]{1,0:T(8,128)(2,1)S(1)}, bf16[1024,256]{1,0:T(8,128)(2,1)S(1)}, u32[]{:S(2)}, u32[]{:S(2)}) %collective-permute-start.3) | collective-permute-done | bytes 524320 | tf_op jit(solution)/shard_map/ppermute | solution.py:37
  35.6 0.2 second_blocks_0.1
  35.8 2.0 %collective-permute-start.4 = (f32[8,128]{1,0:T(8,128)S(1)}, f32[8,128]{1,0:T(8,128)S(1)}, u32[]{:S(2)}, u32[]{:S(2)}) collective-permute-start(f32[8,128]{1,0:T(8,128)S(1)} %get-tuple-element.29), channel_id=1, source_target_pairs={{0,16},{1,17},{2,18},{3,19},{4,20},{5,21},{6,22},{7,23},{8,24},{9,... | collective-permute-start | bytes 12296 | tf_op jit(solution)/shard_map/ppermute | solution.py:250
  37.8 0.8 %collective-permute-done.4.refs_3_ = f32[8,128]{1,0:T(8,128)S(1)} collective-permute-done((f32[8,128]{1,0:T(8,128)S(1)}, f32[8,128]{1,0:T(8,128)S(1)}, u32[]{:S(2)}, u32[]{:S(2)}) %collective-permute-start.4) | collective-permute-done | bytes 4128 | tf_op jit(solution)/shard_map/ppermute | solution.py:250
  38.6 1.1 %collective-permute-start.5 = (bf16[1024,128]{1,0:T(8,128)(2,1)S(1)}, bf16[1024,128]{1,0:T(8,128)(2,1)S(1)}, u32[]{:S(2)}, u32[]{:S(2)}) collective-permute-start(bf16[1024,128]{1,0:T(8,128)(2,1)S(1)} %get-tuple-element.30), channel_id=1, source_target_pairs={{0,2},{1,3},{2,0},{3,1},{4,6},{5,7},{6,4},{7,5},{8,10},{9,11},{10,... | collective-permute-start | bytes 786440 | tf_op jit(solution)/shard_map/ppermute | solution.py:37
  39.7 0.0 collective-permute-done.6.refs_1_
  39.7 0.0 collective-permute-done.7.refs_2_
  39.7 0.2 second_blocks_1.1
  39.9 0.5 collective-permute-start.8
  40.4 2.2 %collective-permute-start.9 = (bf16[1024,128]{1,0:T(8,128)(2,1)S(1)}, bf16[1024,128]{1,0:T(8,128)(2,1)S(1)}, u32[]{:S(2)}, u32[]{:S(2)}) collective-permute-start(bf16[1024,128]{1,0:T(8,128)(2,1)S(1)} %get-tuple-element.35), channel_id=1, source_target_pairs={{0,3},{1,0},{2,1},{3,2},{4,7},{5,4},{6,5},{7,6},{8,11},{9,8},{10,9... | collective-permute-start | bytes 786440 | tf_op jit(solution)/shard_map/ppermute | solution.py:37
  42.6 3.0 %collective-permute-done.5.one = bf16[1024,128]{1,0:T(8,128)(2,1)S(1)} collective-permute-done((bf16[1024,128]{1,0:T(8,128)(2,1)S(1)}, bf16[1024,128]{1,0:T(8,128)(2,1)S(1)}, u32[]{:S(2)}, u32[]{:S(2)}) %collective-permute-start.5) | collective-permute-done | bytes 262176 | tf_op jit(solution)/shard_map/ppermute | solution.py:37
  45.7 2.8 %collective-permute-done.8.two = bf16[1024,128]{1,0:T(8,128)(2,1)S(1)} collective-permute-done((bf16[1024,128]{1,0:T(8,128)(2,1)S(1)}, bf16[1024,128]{1,0:T(8,128)(2,1)S(1)}, u32[]{:S(2)}, u32[]{:S(2)}) %collective-permute-start.8) | collective-permute-done | bytes 262176 | tf_op jit(solution)/shard_map/ppermute | solution.py:37
  48.4 0.0 collective-permute-done.9.three
  48.5 0.0 copy-done
  48.5 1.0 %lift.1 = (bf16[1024,128]{1,0:T(8,128)(2,1)}, f32[128,128]{1,0:T(8,128)S(1)}) custom-call(f32[1024,128]{1,0:T(8,128)S(1)} %get-tuple-element.27.mine, bf16[1024,128]{1,0:T(8,128)(2,1)S(1)} %collective-permute-done.5.one, bf16[1024,128]{1,0:T(8,128)(2,1)S(1)} %collective-permute-done.8.two, bf16[1024,128]{1,0:T(8,128)(2,1)S(1)} %collective-permute-done.9.three, ...), custom_call_target="tpu_custom_call" | custom-call | tf_op jit(solution)/shard_map/lift/pallas_call | solution.py:228
  49.4 18.6 %all_to_all.12 = f32[128,1,128]{2,1,0:T(1,128)S(1)} all-to-all(f32[128,1,128]{2,1,0:T(1,128)S(1)} %bitcast.4), channel_id=1, replica_groups=mesh['row'=8,'col_0'=4,'col_1'=4] {'row','col_0','col_1'}, dimensions={0} | all-to-all | bytes 131072 | tf_op jit(solution)/shard_map/all_to_all | solution.py:257
  68.0 0.5 slice_reduce_fusion
Async XLA Ops:
  8.6 11.9 %collective-permute-start.1 = (bf16[1024,256]{1,0:T(8,128)(2,1)S(1)}, bf16[1024,256]{1,0:T(8,128)(2,1)S(1)}, u32[]{:S(2)}, u32[]{:S(2)}) collective-permute-start(bf16[1024,256]{1,0:T(8,128)(2,1)S(1)} %get-tuple-element.24), channel_id=1, source_target_pairs={{0,12},{1,13},{2,14},{3,15},{4,0},{5,1},{6,2},{7,3},{8,4},{9,5},{1... | collective-permute-start | bytes 1572872 | tf_op jit(solution)/shard_map/ppermute | solution.py:37
  13.2 9.5 %collective-permute-start.2 = (bf16[1024,256]{1,0:T(8,128)(2,1)S(1)}, bf16[1024,256]{1,0:T(8,128)(2,1)S(1)}, u32[]{:S(2)}, u32[]{:S(2)}) collective-permute-start(bf16[1024,256]{1,0:T(8,128)(2,1)S(1)} %get-tuple-element.25), channel_id=1, source_target_pairs={{0,4},{1,5},{2,6},{3,7},{4,8},{5,9},{6,10},{7,11},{8,12},{9,13},{1... | collective-permute-start | bytes 1572872 | tf_op jit(solution)/shard_map/ppermute | solution.py:37
  17.7 17.0 %collective-permute-start = (bf16[1024,256]{1,0:T(8,128)(2,1)S(1)}, bf16[1024,256]{1,0:T(8,128)(2,1)S(1)}, u32[]{:S(2)}, u32[]{:S(2)}) collective-permute-start(bf16[1024,256]{1,0:T(8,128)(2,1)S(1)} %get-tuple-element.22), channel_id=1, source_target_pairs={{0,4},{1,5},{2,6},{3,7},{4,8},{5,9},{6,10},{7,11},{8,12},{9,13},{1... | collective-permute-start | bytes 1572872 | tf_op jit(solution)/shard_map/ppermute | solution.py:37
  17.8 21.9 %collective-permute-start.6 = (bf16[1024,256]{1,0:T(8,128)(2,1)S(1)}, bf16[1024,256]{1,0:T(8,128)(2,1)S(1)}, u32[]{:S(2)}, u32[]{:S(2)}) collective-permute-start(bf16[1024,256]{1,0:T(8,128)(2,1)S(1)} %get-tuple-element.31), channel_id=1, source_target_pairs={{0,12},{1,13},{2,14},{3,15},{4,0},{5,1},{6,2},{7,3},{8,4},{9,5},{1... | collective-permute-start | bytes 1572872 | tf_op jit(solution)/shard_map/ppermute | solution.py:37
  27.2 8.4 %collective-permute-start.3 = (bf16[1024,256]{1,0:T(8,128)(2,1)S(1)}, bf16[1024,256]{1,0:T(8,128)(2,1)S(1)}, u32[]{:S(2)}, u32[]{:S(2)}) collective-permute-start(bf16[1024,256]{1,0:T(8,128)(2,1)S(1)} %get-tuple-element.26), channel_id=1, source_target_pairs={{0,12},{1,13},{2,14},{3,15},{4,0},{5,1},{6,2},{7,3},{8,4},{9,5},{1... | collective-permute-start | bytes 1572872 | tf_op jit(solution)/shard_map/ppermute | solution.py:37
  27.3 21.1 %copy-start = (bf16[1024,128]{1,0:T(8,128)(2,1)S(1)}, bf16[1024,128]{1,0:T(8,128)(2,1)}, u32[]{:S(2)}) copy-start(bf16[1024,128]{1,0:T(8,128)(2,1)} %current.1) | copy-start | bytes 786436
  27.3 12.4 %collective-permute-start.7 = (bf16[1024,256]{1,0:T(8,128)(2,1)S(1)}, bf16[1024,256]{1,0:T(8,128)(2,1)S(1)}, u32[]{:S(2)}, u32[]{:S(2)}) collective-permute-start(bf16[1024,256]{1,0:T(8,128)(2,1)S(1)} %get-tuple-element.32), channel_id=1, source_target_pairs={{0,4},{1,5},{2,6},{3,7},{4,8},{5,9},{6,10},{7,11},{8,12},{9,13},{1... | collective-permute-start | bytes 1572872 | tf_op jit(solution)/shard_map/ppermute | solution.py:37
  35.8 2.8 %collective-permute-start.4 = (f32[8,128]{1,0:T(8,128)S(1)}, f32[8,128]{1,0:T(8,128)S(1)}, u32[]{:S(2)}, u32[]{:S(2)}) collective-permute-start(f32[8,128]{1,0:T(8,128)S(1)} %get-tuple-element.29), channel_id=1, source_target_pairs={{0,16},{1,17},{2,18},{3,19},{4,20},{5,21},{6,22},{7,23},{8,24},{9,... | collective-permute-start | bytes 12296 | tf_op jit(solution)/shard_map/ppermute | solution.py:250
  38.6 7.1 %collective-permute-start.5 = (bf16[1024,128]{1,0:T(8,128)(2,1)S(1)}, bf16[1024,128]{1,0:T(8,128)(2,1)S(1)}, u32[]{:S(2)}, u32[]{:S(2)}) collective-permute-start(bf16[1024,128]{1,0:T(8,128)(2,1)S(1)} %get-tuple-element.30), channel_id=1, source_target_pairs={{0,2},{1,3},{2,0},{3,1},{4,6},{5,7},{6,4},{7,5},{8,10},{9,11},{10,... | collective-permute-start | bytes 786440 | tf_op jit(solution)/shard_map/ppermute | solution.py:37
  39.9 8.6 %collective-permute-start.8 = (bf16[1024,128]{1,0:T(8,128)(2,1)S(1)}, bf16[1024,128]{1,0:T(8,128)(2,1)S(1)}, u32[]{:S(2)}, u32[]{:S(2)}) collective-permute-start(bf16[1024,128]{1,0:T(8,128)(2,1)S(1)} %get-tuple-element.34), channel_id=1, source_target_pairs={{0,1},{1,2},{2,3},{3,0},{4,5},{5,6},{6,7},{7,4},{8,9},{9,10},{10,1... | collective-permute-start | bytes 786440 | tf_op jit(solution)/shard_map/ppermute | solution.py:37
  40.4 8.0 %collective-permute-start.9 = (bf16[1024,128]{1,0:T(8,128)(2,1)S(1)}, bf16[1024,128]{1,0:T(8,128)(2,1)S(1)}, u32[]{:S(2)}, u32[]{:S(2)}) collective-permute-start(bf16[1024,128]{1,0:T(8,128)(2,1)S(1)} %get-tuple-element.35), channel_id=1, source_target_pairs={{0,3},{1,0},{2,1},{3,2},{4,7},{5,4},{6,5},{7,6},{8,11},{9,8},{10,9... | collective-permute-start | bytes 786440 | tf_op jit(solution)/shard_map/ppermute | solution.py:37
